TPU v7x, 128 devices: a whole 4x4x4 slice. The times are simulated.
128 devices in a mesh: outer: 8 (over y, core), inner: 4 (over z), head: 4 (over x).
Axes of the slice: x: 4, y: 4, z: 4, core: 2. Of those that a mesh axis runs over, the one named last changes fastest.
Arguments:
- queries: bfloat16 [32768, 4096], P(('outer', 'inner'), 'head'), may hold values from -6 to 6
- keys: bfloat16 [32768, 4096], P(('outer', 'inner'), 'head'), may hold values from -0.046875 to 0.046875
- values: bfloat16 [32768, 4096], P(('outer', 'inner'), 'head'), may hold values from -36 to 36
- out_grad: bfloat16 [32768, 4096], P(('outer', 'inner'), 'head'), may hold values from -6 to 6
- log_key_decay: float32 [32768, 4096], P(('outer', 'inner'), 'head'), may hold values from -0.62 to 0
- value_rate: float32 [4096], P('head'), may hold values from 3.0517579e-06 to 0.05
- norm_gain: float32 [4096], P('head'), may hold values from 0.1 to 1.9
Outputs:
- query_grad: bfloat16 [32768, 4096], P(('outer', 'inner'), 'head')
- key_grad: bfloat16 [32768, 4096], P(('outer', 'inner'), 'head')
- value_grad: bfloat16 [32768, 4096], P(('outer', 'inner'), 'head')
- gain_grad: float32 [4096], P('head')
All inputs are finite; a program needn't handle non-finite values.
Results may differ from a plain program's by a relative error of at most 0.001.
Values sent between devices are 32-bit elements; how exact they have to be, the bound alone decides.
No kernel may reach another device: no remote copies, remote signals or barrier semaphores. Data moves between devices by JAX's collectives and lax.ppermute only.
A program may use at most 192 MiB of HBM per device.

v0:
```python
import functools
import math

import jax
import jax.numpy as jnp
from jax import lax
from jax.experimental import pallas as pl
from jax.experimental.pallas import tpu as pltpu
from jax.sharding import PartitionSpec as P

HEADS = 32
D = 128
BL = 128
HALF = BL // 2
EXTRA = 8
VMEM_MIB = 56
TOGETHER = 2
f32 = jnp.float32
bf16 = jnp.bfloat16

NN = (((1,), (0,)), ((), ()))
NT = (((1,), (1,)), ((), ()))
TN = (((0,), (0,)), ((), ()))


def dot(a, b, dims):
    return lax.dot_general(a, b, dims, preferred_element_type=f32)


def pack(x):
    high = x.astype(bf16)
    return jnp.concatenate([high, (x - high.astype(f32)).astype(bf16)], axis=1)


def halves(x):
    return x[:, :D] + x[:, D:]


def nn(a, b):
    return halves(dot(a, jnp.concatenate([b, b], axis=0), NN))


def nt(a, b):
    high, low = b[:, :D], b[:, D:]
    rows_high = jnp.concatenate([high, high], axis=1)
    rows_low = jnp.concatenate([low, low], axis=1)
    return halves(dot(a, jnp.concatenate([rows_high, rows_low], axis=0), NT))


def tn(a, b):
    stacked = jnp.concatenate([a[:, :D], a[:, D:]], axis=0)
    return halves(dot(stacked, jnp.concatenate([b, b], axis=0), TN))


def tn_long(a, b):
    x = dot(a, b, TN)
    return halves(x[:D] + x[D:])


def iota(axis):
    return lax.broadcasted_iota(jnp.int32, (BL, BL), axis)


def causal():
    return iota(0) >= iota(1)


def centred_sum_matrix():
    t, s = iota(0), iota(1)
    later = ((s <= t) & (s >= HALF)).astype(f32)
    earlier = ((s > t) & (s < HALF)).astype(f32)
    return (later - earlier).astype(bf16)


def rows(b):
    return slice(b * BL, (b + 1) * BL)


def value_tables(value_log):
    steps = (iota(0) - (HALF - 1)).astype(f32) * value_log
    return jnp.exp(steps), jnp.exp(-steps)


def cols(h, width=D):
    return slice(h * width, (h + 1) * width)


def last_row(b):
    return slice((b + 1) * BL - 1, (b + 1) * BL)


def before_and_after(c_ref, mid_ref, h, blocks):
    ends = [c_ref[last_row(b), cols(h)] for b in range(blocks)]
    mids = [mid_ref[h, b : b + 1] for b in range(blocks)]
    before, total = [], jnp.zeros((1, D), f32)
    for b in range(blocks):
        before.append(total + mids[b])
        total = before[b] + ends[b]
    after, rest = [None] * blocks, jnp.zeros((1, D), f32)
    for b in reversed(range(blocks)):
        after[b] = rest + ends[b]
        rest = after[b] + mids[b]
    steps = [jnp.exp(ends[b] + mids[b + 1]) for b in range(blocks - 1)]
    return before, after, steps


def columns_of(row_list):
    stacked = jnp.concatenate(row_list, axis=0)
    padded = jnp.concatenate([stacked, jnp.zeros((D - stacked.shape[0], D), f32)], axis=0)
    return jnp.transpose(padded)


def centred_sums(blocks, ld_ref, c_ref, h):
    matrix = centred_sum_matrix()
    matrix = jnp.concatenate([matrix, matrix], axis=1)
    mids = []
    for b in range(0, blocks, 2):
        x, y = pack(ld_ref[rows(b), cols(h)]), pack(ld_ref[rows(b + 1), cols(h)])
        right = jnp.concatenate(
            [
                jnp.concatenate([x[:, :D], y[:, :D]], axis=1),
                jnp.concatenate([x[:, D:], y[:, D:]], axis=1),
            ],
            axis=0,
        )
        c = dot(matrix, right, NN)
        for at in range(2):
            c_at = c[:, cols(at)]
            c_ref[rows(b + at), cols(h)] = c_at
            first = (b + at) * BL
            mids.append(ld_ref[first : first + 1, cols(h)] - c_at[0:1])
    return mids


def state_kernel(blocks, k_ref, v_ref, ld_ref, rate_ref, pay_ref, c_s, kk, vv):
    span = blocks * BL
    all_mids = [centred_sums(blocks, ld_ref, c_s, h) for h in range(TOGETHER)]
    for h in range(TOGETHER):
        value_log = -rate_ref[h]
        _, shrink = value_tables(value_log)
        rest = jnp.zeros((1, D), f32)
        for b in reversed(range(blocks)):
            c = c_s[rows(b), cols(h)]
            after = rest + c[BL - 1 : BL]
            rest = after + all_mids[h][b]
            kk[h, rows(b)] = pack(k_ref[rows(b), cols(h)].astype(f32) * jnp.exp(after - c))
            reach = jnp.exp(value_log * float(span - BL * b - HALF))
            vv[h, rows(b)] = pack(v_ref[rows(b), cols(h)].astype(f32) * (shrink * reach))
        total = tn_long(kk[h], vv[h])
        value_total = value_log * float(span)
        for part in range(4):
            pay_ref[4 * h + part, 0:32] = total[32 * part : 32 * part + 32]
            pay_ref[4 * h + part, 32:40] = jnp.concatenate(
                [pltpu.roll(rest, (D - 32 * part) % D, 1), value_total, jnp.zeros((6, D), f32)],
                axis=0,
            )


def local_kernel(
    blocks, q_ref, k_ref, v_ref, ld_ref, rate_ref,
    core_ref, qd_ref, starts_ref, c_ref, mid_ref, qs, ks, vs, scores, kv,
):
    mask = causal()
    tables = []
    for h in range(TOGETHER):
        mids = centred_sums(blocks, ld_ref, c_ref, h)
        mid_ref[h] = jnp.concatenate(mids, axis=0)
    for h in range(TOGETHER):
        grow, shrink = value_tables(-rate_ref[h])
        before, _, steps = before_and_after(c_ref, mid_ref, h, blocks)
        tables.append((grow, steps))
        for b in range(blocks):
            c = c_ref[rows(b), cols(h)]
            q = q_ref[rows(b), cols(h)].astype(f32) * jnp.exp(c)
            qs[h, rows(b)] = pack(q)
            qd_ref[rows(b), cols(h, 2 * D)] = pack(q * jnp.exp(before[b]))
            ks[h, rows(b)] = pack(k_ref[rows(b), cols(h)].astype(f32) * jnp.exp(-c))
            vs[h, rows(b)] = pack(v_ref[rows(b), cols(h)].astype(f32) * shrink)
    for h in range(TOGETHER):
        for b in range(blocks):
            part = nt(qs[h, rows(b)], ks[h, rows(b)])
            scores[h, rows(b)] = pack(jnp.where(mask, part, 0.0))
    for h in range(TOGETHER):
        for b in range(blocks - 1):
            kv[h, b] = tn(ks[h, rows(b)], vs[h, rows(b)])
    for h in range(TOGETHER):
        key_steps = columns_of(tables[h][1])
        value_step = jnp.exp(-rate_ref[h] * float(BL))
        state = jnp.zeros((D, D), f32)
        for b in range(blocks):
            starts_ref[h, b] = state
            if b < blocks - 1:
                state = (state + kv[h, b]) * (key_steps[:, b : b + 1] * value_step)
    for h in range(TOGETHER):
        for b in range(blocks):
            value, state = vs[h, rows(b)], pack(starts_ref[h, b])
            left = jnp.concatenate([scores[h, rows(b)], qs[h, rows(b)]], axis=1)
            right = jnp.concatenate([value, value, state, state], axis=0)
            core_ref[rows(b), cols(h)] = tables[h][0] * halves(dot(left, right, NN))


def core_kernel(
    blocks, turns, qd_ref, local_ref, grad_ref, state_ref, rate_ref, gain_ref,
    core_ref, sums_ref, squares, crosses,
):
    turn = pl.program_id(0)

    @pl.when(turn == 0)
    def _():
        squares[...] = jnp.zeros_like(squares)
        crosses[...] = jnp.zeros_like(crosses)

    grows, rights = [], []
    for h in range(TOGETHER):
        grows.append(value_tables(-rate_ref[h])[0])
        state = pack(state_ref[h])
        rights.append(jnp.concatenate([state, state], axis=0))
    for b in range(blocks):
        square, cross = squares[rows(b)], crosses[rows(b)]
        for h in range(TOGETHER):
            reach = jnp.exp(-rate_ref[h] * float(BL * b + HALF))
            incoming = halves(dot(qd_ref[rows(b), cols(h, 2 * D)], rights[h], NN))
            core = local_ref[rows(b), cols(h)] + (grows[h] * reach) * incoming
            core_ref[rows(b), cols(h)] = core
            square = square + core * core
            cross = cross + core * (grad_ref[rows(b), cols(h)].astype(f32) * gain_ref[h])
        squares[rows(b)] = square
        crosses[rows(b)] = cross

    @pl.when(turn == turns - 1)
    def _():
        ones = jnp.ones((8, 2 * D), bf16)
        for at, ref in enumerate((squares, crosses)):
            found = [dot(ones, pack(ref[rows(b)]), NT)[0:1] for b in range(blocks)]
            all_found = jnp.concatenate(found, axis=0)
            for copy in range(sums_ref.shape[0]):
                sums_ref[copy, at * blocks : (at + 1) * blocks] = all_found


def grad_kernel(
    blocks, qd_ref, core_ref, grad_ref, sums_ref, rate_ref, gain_ref, pay_ref, factor_ref, gg
):
    turn = pl.program_id(0)
    columns = HEADS * D

    @pl.when(turn == 0)
    def _():
        both = sums_ref[0]
        for copy in range(1, sums_ref.shape[0]):
            both = both + sums_ref[copy]
        rms = lax.rsqrt(both[0:blocks] / columns + 1e-06)
        coef = rms * rms * rms * both[blocks : 2 * blocks] / columns
        for b in range(blocks):
            factor_ref[rows(b), :D] = jnp.transpose(jnp.broadcast_to(rms[b : b + 1], (BL, D)))
            factor_ref[rows(b), D:] = jnp.transpose(jnp.broadcast_to(coef[b : b + 1], (BL, D)))

    for h in range(TOGETHER):
        grow, _ = value_tables(-rate_ref[h])
        gain_sum = jnp.zeros((BL, D), f32)
        for b in range(blocks):
            core = core_ref[rows(b), cols(h)]
            out = grad_ref[rows(b), cols(h)].astype(f32) * factor_ref[rows(b), :D]
            gain_sum = gain_sum + out * core
            g = out * gain_ref[h] - core * factor_ref[rows(b), D:]
            reach = jnp.exp(-rate_ref[h] * float(BL * b + HALF))
            gg[h, rows(b)] = pack(g * (grow * reach))
        total = tn_long(qd_ref[:, cols(h, 2 * D)], gg[h])
        gain_row = jnp.sum(gain_sum, axis=0, keepdims=True)
        for part in range(4):
            pay_ref[4 * h + part, 0:32] = total[32 * part : 32 * part + 32]
            pay_ref[4 * h + part, 32:40] = jnp.concatenate(
                [gain_row, jnp.zeros((7, D), f32)], axis=0
            )


def block_grad_kernel(
    blocks, made, q_ref, k_ref, v_ref, c_ref, mid_ref, core_ref, grad_ref, factor_ref,
    starts_ref, state_ref, rate_ref, gain_ref, *rest,
):
    dq_ref, dk_ref, dv_ref, qs, ks, vs, gs, start, mixed, scores, qg, passed = rest[made:]
    mask = causal()
    tables = []
    for h in range(TOGETHER):
        grow, shrink = value_tables(-rate_ref[h])
        before, _, steps = before_and_after(c_ref, mid_ref, h, blocks)
        key_columns = columns_of(steps + [jnp.exp(x) for x in before])
        tables.append((shrink, key_columns))
        for b in range(blocks):
            c = c_ref[rows(b), cols(h)]
            qs[h, rows(b)] = pack(q_ref[rows(b), cols(h)].astype(f32) * jnp.exp(c))
            ks[h, rows(b)] = pack(k_ref[rows(b), cols(h)].astype(f32) * jnp.exp(-c))
            vs[h, rows(b)] = pack(v_ref[rows(b), cols(h)].astype(f32) * shrink)
            out = grad_ref[rows(b), cols(h)].astype(f32) * factor_ref[rows(b), :D]
            g = out * gain_ref[h] - core_ref[rows(b), cols(h)] * factor_ref[rows(b), D:]
            gs[h, rows(b)] = pack(g * grow)
            at = blocks - 1 + b
            reach = jnp.exp(-rate_ref[h] * float(BL * b + HALF))
            begun = starts_ref[h, b] + state_ref[h] * (key_columns[:, at : at + 1] * reach)
            start[h, rows(b)] = pack(begun)
    for h in range(TOGETHER):
        for b in range(blocks):
            part = nt(gs[h, rows(b)], vs[h, rows(b)])
            mixed[h, rows(b)] = pack(jnp.where(mask, part, 0.0))
            part = nt(qs[h, rows(b)], ks[h, rows(b)])
            scores[h, rows(b)] = pack(jnp.where(mask, part, 0.0))
    for h in range(TOGETHER):
        for b in range(1, blocks):
            qg[h, b] = tn(qs[h, rows(b)], gs[h, rows(b)])
    for h in range(TOGETHER):
        value_step = jnp.exp(-rate_ref[h] * float(BL))
        now = jnp.zeros((D, D), f32)
        for b in reversed(range(blocks)):
            passed[h, rows(b)] = pack(now)
            if b:
                now = (now + qg[h, b]) * (tables[h][1][:, b - 1 : b] * value_step)
    for h in range(TOGETHER):
        for b in range(blocks):
            dq = nn(mixed[h, rows(b)], ks[h, rows(b)]) + nt(gs[h, rows(b)], start[h, rows(b)])
            dq_ref[rows(b), cols(h)] = (jnp.exp(c_ref[rows(b), cols(h)]) * dq).astype(bf16)
    for h in range(TOGETHER):
        for b in range(blocks):
            dk = tn(mixed[h, rows(b)], qs[h, rows(b)]) + nt(vs[h, rows(b)], passed[h, rows(b)])
            dk_ref[rows(b), cols(h)] = jnp.exp(-c_ref[rows(b), cols(h)]) * dk
    for h in range(TOGETHER):
        for b in range(blocks):
            dv = tn(scores[h, rows(b)], gs[h, rows(b)]) + nn(ks[h, rows(b)], passed[h, rows(b)])
            dv_ref[rows(b), cols(h)] = tables[h][0] * dv


def final_kernel(
    blocks, k_ref, v_ref, c_ref, mid_ref, dk_ref, dv_ref, back_ref, rate_ref,
    dk_out, dv_out, gain_out,
):
    span = blocks * BL
    for h in range(TOGETHER):
        value_log = -rate_ref[h]
        _, shrink = value_tables(value_log)
        _, after, _ = before_and_after(c_ref, mid_ref, h, blocks)
        back = pack(back_ref[4 * h : 4 * h + 4, 0:32].reshape(D, D))
        for b in range(blocks):
            at = rows(b), cols(h)
            fade = jnp.exp(after[b] - c_ref[at])
            value_fade = shrink * jnp.exp(value_log * float(span - BL * b - HALF))
            ks = pack(k_ref[at].astype(f32) * fade)
            vs = pack(v_ref[at].astype(f32) * value_fade)
            dk_out[at] = (dk_ref[at] + fade * nt(vs, back)).astype(bf16)
            dv_out[at] = (dv_ref[at] + value_fade * nn(ks, back)).astype(bf16)
        gain_out[h] = back_ref[4 * h, 32:33]


def forward_scan_kernel(count, pay_ref, out_ref, weight_ref):
    decays = jnp.concatenate([pay_ref[s, 32:33] for s in range(count)], axis=0)
    padded = jnp.concatenate([decays, jnp.zeros((D - count, D), f32)], axis=0)
    key_columns = jnp.exp(jnp.transpose(padded)[0:32])
    value_row = jnp.exp(pay_ref[0, 33:34])
    state = jnp.zeros((32, D), f32)
    for s in range(count):
        out_ref[s] = state
        weight = key_columns[:, s : s + 1] * value_row
        weight_ref[s] = weight
        state = weight * state + pay_ref[s, 0:32]


def backward_scan_kernel(count, scale, pay_ref, weight_ref, out_ref):
    state = jnp.zeros((32, D), f32)
    gain = jnp.zeros((EXTRA, D), f32)
    for s in range(count):
        gain = gain + pay_ref[s, 32:40]
    gain = gain * scale
    for s in reversed(range(count)):
        out_ref[s, 0:32] = state
        out_ref[s, 32:40] = gain
        state = weight_ref[s] * state + pay_ref[s, 0:32]


def on_device(queries, keys, values, out_grad, log_key_decay, value_rate, norm_gain):
    tokens, width = queries.shape
    heads = width // D
    blocks = tokens // BL
    around = ("outer", "inner")
    count = lax.axis_size("outer") * lax.axis_size("inner")
    head_count = lax.axis_size("head")
    rate = value_rate.reshape(heads, 1, D)
    gain = norm_gain.reshape(heads, 1, D)
    chunks = heads * 4

    turns = heads // TOGETHER

    def specs(first):
        wide = pl.BlockSpec((tokens, TOGETHER * D), lambda h: (0, h + first))
        pair = pl.BlockSpec((tokens, TOGETHER * 2 * D), lambda h: (0, h + first))
        row = pl.BlockSpec((TOGETHER, 1, D), lambda h: (h + first, 0, 0))
        eight = pl.BlockSpec((TOGETHER, blocks, D), lambda h: (h + first, 0, 0))
        square = pl.BlockSpec((TOGETHER, D, D), lambda h: (h + first, 0, 0))
        many = pl.BlockSpec((TOGETHER, blocks, D, D), lambda h: (h + first, 0, 0, 0))
        payload = pl.BlockSpec((TOGETHER * 4, 32 + EXTRA, D), lambda h: (h + first, 0, 0))
        return wide, pair, row, eight, square, many, payload

    wide, pair, row, eight, square, many, payload = specs(0)
    factors = pl.BlockSpec((tokens, 2 * D), lambda h: (0, 0))
    packed = pltpu.VMEM((TOGETHER, tokens, 2 * D), bf16)
    squares = pltpu.VMEM((TOGETHER, blocks, D, D), f32)
    sums_spec = pl.BlockSpec((head_count, 2 * blocks, D), lambda h: (0, 0, 0))

    def shape(*dims, dtype=f32):
        return jax.ShapeDtypeStruct(dims, dtype)

    wide_shape = shape(tokens, width)
    wide_low = shape(tokens, width, dtype=bf16)
    pair_shape = shape(tokens, 2 * width, dtype=bf16)
    pay_shape = shape(chunks, 32 + EXTRA, D)
    params = pltpu.CompilerParams(
        dimension_semantics=("arbitrary",), vmem_limit_bytes=VMEM_MIB * 1024 * 1024
    )

    def call(body, name, ins, outs, out_shape, scratch=(), flops=0, steps=turns, aliases={}):
        return pl.pallas_call(
            body, name=name, grid=(steps,), in_specs=ins, out_specs=outs, out_shape=out_shape,
            scratch_shapes=list(scratch), compiler_params=params, input_output_aliases=aliases,
            cost_estimate=pl.CostEstimate(
                flops=flops, transcendentals=0, bytes_accessed=16 * 1024 * 1024
            ),
        )

    pay = call(
        functools.partial(state_kernel, blocks), "state", [wide, wide, wide, row],
        payload, pay_shape,
        [pltpu.VMEM((tokens, TOGETHER * D), f32), packed, packed],
    )(keys, values, log_key_decay, rate)
    got = lax.all_to_all(pay, around, 0, 0)
    local, qd, starts, c, mid = call(
        functools.partial(local_kernel, blocks), "local",
        [wide, wide, wide, wide, row], [wide, pair, many, wide, eight],
        [
            wide_shape, pair_shape, shape(heads, blocks, D, D), wide_shape,
            shape(heads, blocks, D),
        ],
        [packed, packed, packed, packed, squares], flops=10**10,
    )(queries, keys, values, log_key_decay, rate)
    prefixes, weights = pl.pallas_call(
        functools.partial(forward_scan_kernel, count), name="fscan",
        out_shape=[shape(chunks, 32, D), shape(chunks, 32, D)],
    )(got)
    state_in = lax.all_to_all(prefixes, around, 0, 0).reshape(heads, D, D)
    core, sums = call(
        functools.partial(core_kernel, blocks, turns), "core",
        [pair, wide, wide, square, row, row], [wide, sums_spec],
        [wide_shape, shape(head_count, 2 * blocks, D)],
        [pltpu.VMEM((tokens, D), f32)] * 2,
    )(qd, local, out_grad, state_in, rate, gain)
    all_sums = lax.all_to_all(sums, "head", 0, 0)
    back_pay, factor = call(
        functools.partial(grad_kernel, blocks), "grad",
        [pair, wide, wide, sums_spec, row, row], [payload, factors],
        [pay_shape, shape(tokens, 2 * D)], [packed],
    )(qd, core, out_grad, all_sums, rate, gain)
    back_got = lax.all_to_all(back_pay, around, 0, 0)
    half = turns // 2
    made = ()
    for part in range(2):
        w, _, r, e, s, m, _ = specs(part * half)
        made = call(
            functools.partial(block_grad_kernel, blocks, len(made)), f"blockgrad{part}",
            [w, w, w, w, e, w, w, factors, m, s, r, r]
            + [pl.BlockSpec(memory_space=pl.ANY)] * len(made),
            [w, w, w], [wide_low, wide_shape, wide_shape],
            [packed] * 7 + [squares, packed], flops=10**10, steps=half,
            aliases={12 + i: i for i in range(len(made))},
        )(
            queries, keys, values, c, mid, core, out_grad, factor, starts, state_in, rate, gain,
            *made,
        )
    dq, dk_local, dv_local = made
    scale = 1.0 / math.sqrt(tokens * count)
    back_prefixes = pl.pallas_call(
        functools.partial(backward_scan_kernel, count, scale), name="bscan", out_shape=pay_shape,
    )(back_got, weights)
    back_in = lax.all_to_all(back_prefixes, around, 0, 0)
    dk, dv, gain_grad = call(
        functools.partial(final_kernel, blocks), "final",
        [wide, wide, wide, eight, wide, wide, payload, row], [wide, wide, row],
        [wide_low, wide_low, shape(heads, 1, D)],
    )(keys, values, c, mid, dk_local, dv_local, back_in, rate)
    return dq, dk, dv, gain_grad.reshape(width)


def solution(mesh):
    spec = P(("outer", "inner"), "head")
    return jax.shard_map(
        on_device,
        mesh=mesh,
        in_specs=(spec, spec, spec, spec, spec, P("head"), P("head")),
        out_specs=(spec, spec, spec, P("head")),
        check_vma=False,
    )
```

profile of v0, /device:TPU:1, one launch (start us, length us, event | category | flops | bytes accessed | tf_op | source)
XLA Modules:
  0.0 131.8 jit_solution(8188389017142225515)
XLA Ops:
  0.6 7.2 %state.1 = f32[32,40,128]{2,1,0:T(8,128)} custom-call(bf16[1024,1024]{1,0:T(8,128)(2,1)} %k_ref.9, bf16[1024,1024]{1,0:T(8,128)(2,1)} %v_ref.9, f32[1024,1024]{1,0:T(8,128)} %ld_ref.3, f32[8,1,128]{2,1,0:T(1,128)} %bitcast.7), custom_call_target="tpu_custom_call" | custom-call | bytes 16777216 | tf_op jit(solution)/shard_map/state/pallas_call | solution.py:425
  7.8 21.9 %all_to_all.25.pay_ref = f32[32,40,128]{2,1,0:T(8,128)} all-to-all(f32[32,40,128]{2,1,0:T(8,128)} %state.1), channel_id=1, replica_groups=mesh['outer'=8,'inner'=4,'head'=4] {'outer','inner'}, dimensions={0} | all-to-all | bytes 1310720 | tf_op jit(solution)/shard_map/all_to_all | solution.py:430
  29.7 2.4 %fscan.1 = (f32[32,32,128]{2,1,0:T(8,128)}, f32[32,32,128]{2,1,0:T(8,128)}) custom-call(f32[32,40,128]{2,1,0:T(8,128)} %all_to_all.25.pay_ref), custom_call_target="tpu_custom_call" | custom-call | tf_op jit(solution)/shard_map/fscan/pallas_call | solution.py:440
  32.1 4.7 %all-to-all-start.1 = ((f32[32,32,128]{2,1,0:T(8,128)}), f32[32,32,128]{2,1,0:T(8,128)S(1)}, u32[]{:S(2)}, u32[]{:S(2)}) async-start(f32[32,32,128]{2,1,0:T(8,128)} %get-tuple-element.28), calls=%async_computation.1 | async-start | bytes 1048576 | tf_op jit(solution)/shard_map/all_to_all | solution.py:444
  36.8 13.3 %local.1 = (f32[1024,1024]{1,0:T(8,128)}, bf16[1024,2048]{1,0:T(8,128)(2,1)}, f32[8,8,128,128]{3,2,1,0:T(8,128)}, f32[1024,1024]{1,0:T(8,128)}, f32[8,8,128]{2,1,0:T(8,128)}) custom-call(bf16[1024,1024]{1,0:T(8,128)(2,1)} %q_ref.5, bf16[1024,1024]{1,0:T(8,128)(2,1)} %k_ref.9, bf16[1024,1024]{1,0:T(8,128)(2,1)} %v_ref.9, f32[1024,1024]{1,0:T(8,128)} %ld_ref.3, ...), custom_call_target="tpu_custom_call" | custom-call | flops 10000000000 | bytes 16777216 | tf_op jit(solution)/shard_map/local/pallas_call | solution.py:431
  50.1 0.0 all-to-all-done.1
  50.1 0.0 copy-start.2
  50.1 0.8 copy-done.2
  50.9 7.8 %core.1 = (f32[1024,1024]{1,0:T(8,128)}, f32[4,16,128]{2,1,0:T(8,128)}) custom-call(bf16[1024,2048]{1,0:T(8,128)(2,1)} %get-tuple-element.26.qd_ref, f32[1024,1024]{1,0:T(8,128)} %get-tuple-element.27.local_ref, bf16[1024,1024]{1,0:T(8,128)(2,1)} %grad_ref.7, f32[8,128,128]{2,1,0:T(8,128)} %bitcast.4, f32[8,1,128]{2,1,0:T(1,128)} %bitcast.9, ...), custom_call_target="tpu_custom_call" | custom-call | bytes 16777216 | tf_op jit(solution)/shard_map/core/pallas_call | solution.py:445
  58.7 8.4 %all_to_all.26.sums_ref = f32[4,16,128]{2,1,0:T(8,128)} all-to-all(f32[4,16,128]{2,1,0:T(8,128)} %get-tuple-element.30), channel_id=1, replica_groups=mesh['outer'=8,'inner'=4,'head'=4] {'head'}, dimensions={0} | all-to-all | bytes 65536 | tf_op jit(solution)/shard_map/all_to_all | solution.py:451
  67.1 7.3 %grad.1 = (f32[32,40,128]{2,1,0:T(8,128)}, f32[1024,256]{1,0:T(8,128)}) custom-call(bf16[1024,2048]{1,0:T(8,128)(2,1)} %get-tuple-element.26.qd_ref, f32[1024,1024]{1,0:T(8,128)} %get-tuple-element.29.core_ref, bf16[1024,1024]{1,0:T(8,128)(2,1)} %grad_ref.7, f32[4,16,128]{2,1,0:T(8,128)} %all_to_all.26.sums_ref, f32[8,1,128]{2,1,0:T(1,128)} %bitcast.10, ...), custom_call_target="tpu_custom_call" | custom-call | bytes 16777216 | tf_op jit(solution)/shard_map/grad/pallas_call | solution.py:452
  74.4 8.9 %all-to-all-start.3 = ((f32[32,40,128]{2,1,0:T(8,128)}), f32[32,40,128]{2,1,0:T(8,128)S(1)}, u32[]{:S(2)}, u32[]{:S(2)}) async-start(f32[32,40,128]{2,1,0:T(8,128)} %get-tuple-element.39), calls=%async_computation.3 | async-start | bytes 1310720 | tf_op jit(solution)/shard_map/all_to_all | solution.py:457
  83.3 13.7 %blockgrad0.1 = (bf16[1024,1024]{1,0:T(8,128)(2,1)}, f32[1024,1024]{1,0:T(8,128)}, f32[1024,1024]{1,0:T(8,128)}) custom-call(bf16[1024,1024]{1,0:T(8,128)(2,1)} %q_ref.5, bf16[1024,1024]{1,0:T(8,128)(2,1)} %k_ref.9, bf16[1024,1024]{1,0:T(8,128)(2,1)} %v_ref.9, f32[1024,1024]{1,0:T(8,128)} %get-tuple-element.24.c_ref, ...), custom_call_target="tpu_custom_call" | custom-call | flops 10000000000 | bytes 16777216 | tf_op jit(solution)/shard_map/blockgrad0/pallas_call | solution.py:462
  97.0 0.0 all-to-all-done.3.pay_ref
  97.0 0.0 copy-start.1
  97.0 0.8 copy-done.1
  97.8 2.2 %bscan.1 = f32[32,40,128]{2,1,0:T(8,128)} custom-call(f32[32,40,128]{2,1,0:T(8,128)} %copy-done.1, f32[32,32,128]{2,1,0:T(8,128)} %get-tuple-element.40.weight_ref), custom_call_target="tpu_custom_call" | custom-call | tf_op jit(solution)/shard_map/bscan/pallas_call | solution.py:475
  100.0 7.4 %all-to-all-start.4 = ((f32[32,40,128]{2,1,0:T(8,128)}), f32[32,40,128]{2,1,0:T(8,128)S(1)}, u32[]{:S(2)}, u32[]{:S(2)}) async-start(f32[32,40,128]{2,1,0:T(8,128)} %bscan.1), calls=%async_computation.4 | async-start | bytes 1310720 | tf_op jit(solution)/shard_map/all_to_all | solution.py:478
  107.4 13.7 %blockgrad1.1 = (bf16[1024,1024]{1,0:T(8,128)(2,1)}, f32[1024,1024]{1,0:T(8,128)}, f32[1024,1024]{1,0:T(8,128)}) custom-call(bf16[1024,1024]{1,0:T(8,128)(2,1)} %q_ref.5, bf16[1024,1024]{1,0:T(8,128)(2,1)} %k_ref.9, bf16[1024,1024]{1,0:T(8,128)(2,1)} %v_ref.9, ...), custom_call_target="tpu_custom_call", output_to_operand_aliasing={{0}: (12, {}), {1}: (13, {}), {2}: (14, {})} | custom-call | flops 10000000000 | bytes 16777216 | tf_op jit(solution)/shard_map/blockgrad1/pallas_call | solution.py:462
  121.0 0.0 all-to-all-done.4.back_ref
  121.0 0.0 copy-start
  121.1 0.8 copy-done
  121.9 9.8 %final.1 = (bf16[1024,1024]{1,0:T(8,128)(2,1)}, bf16[1024,1024]{1,0:T(8,128)(2,1)}, f32[8,1,128]{2,1,0:T(1,128)}) custom-call(bf16[1024,1024]{1,0:T(8,128)(2,1)} %k_ref.9, bf16[1024,1024]{1,0:T(8,128)(2,1)} %v_ref.9, f32[1024,1024]{1,0:T(8,128)} %get-tuple-element.24.c_ref, f32[8,8,128]{2,1,0:T(8,128)} %get-tuple-element.25.mid_ref, ...), custom_call_target="tpu_custom_call" | custom-call | bytes 16777216 | tf_op jit(solution)/shard_map/final/pallas_call | solution.py:479
Async XLA Ops:
  32.1 18.0 %all-to-all-start.1 = ((f32[32,32,128]{2,1,0:T(8,128)}), f32[32,32,128]{2,1,0:T(8,128)S(1)}, u32[]{:S(2)}, u32[]{:S(2)}) async-start(f32[32,32,128]{2,1,0:T(8,128)} %get-tuple-element.28), calls=%async_computation.1 | async-start | bytes 1048576 | tf_op jit(solution)/shard_map/all_to_all | solution.py:444
  50.1 0.8 copy-start.2
  74.4 22.6 %all-to-all-start.3 = ((f32[32,40,128]{2,1,0:T(8,128)}), f32[32,40,128]{2,1,0:T(8,128)S(1)}, u32[]{:S(2)}, u32[]{:S(2)}) async-start(f32[32,40,128]{2,1,0:T(8,128)} %get-tuple-element.39), calls=%async_computation.3 | async-start | bytes 1310720 | tf_op jit(solution)/shard_map/all_to_all | solution.py:457
  97.0 0.8 copy-start.1
  100.0 21.1 %all-to-all-start.4 = ((f32[32,40,128]{2,1,0:T(8,128)}), f32[32,40,128]{2,1,0:T(8,128)S(1)}, u32[]{:S(2)}, u32[]{:S(2)}) async-start(f32[32,40,128]{2,1,0:T(8,128)} %bscan.1), calls=%async_computation.4 | async-start | bytes 1310720 | tf_op jit(solution)/shard_map/all_to_all | solution.py:478
  121.0 0.8 copy-start
where the time goes:
time: 133 us; the launch traced here: 132 us
  Pallas kernels  77.2 us (58%)
  blocking collectives  30.3 us (23%)
  starting transfers between devices  21 us (16%)
  local copies, waits for them, and re-layouts  2.46 us (2%)
    pallas_call x2, Pallas kernels, on_device(): call(functools.partial(block_grad_kernel, blocks, len(made)), f'blockgrad...  27.3 us
    all_to_all x1, blocking collectives, on_device(): got = lax.all_to_all(pay, around, 0, 0)  21.9 us
    pallas_call x1, Pallas kernels, on_device(): call(functools.partial(local_kernel, blocks), 'local', [wide, wide, wide,...  13.3 us
    pallas_call x1, Pallas kernels, on_device(): call(functools.partial(final_kernel, blocks), 'final', [wide, wide, wide,...  9.79 us
    all_to_all x1, starting transfers between devices, on_device(): back_got = lax.all_to_all(back_pay, around, 0, 0)  8.88 us
    all_to_all x1, blocking collectives, on_device(): all_sums = lax.all_to_all(sums, 'head', 0, 0)  8.41 us
    pallas_call x1, Pallas kernels, on_device(): call(functools.partial(core_kernel, blocks, turns), 'core', [pair, wide,...  7.79 us
    all_to_all x1, starting transfers between devices, on_device(): back_in = lax.all_to_all(back_prefixes, around, 0, 0)  7.38 us
  transfers between devices with their start and end apart: 3, of which 0 were waited for; matrix products, arithmetic and copies ran while one was open for 0% of the time, Pallas kernels for 31%

commit v1 on v0

--- a/solution.py
+++ b/solution.py
@@ -157,9 +157,9 @@
 
 
 def local_kernel(
-    blocks, q_ref, k_ref, v_ref, ld_ref, rate_ref,
-    core_ref, qd_ref, starts_ref, c_ref, mid_ref, qs, ks, vs, scores, kv,
+    blocks, made, q_ref, k_ref, v_ref, ld_ref, rate_ref, *rest
 ):
+    core_ref, qd_ref, starts_ref, c_ref, mid_ref, qs, ks, vs, scores, kv = rest[made:]
     mask = causal()
     tables = []
     for h in range(TOGETHER):
@@ -172,17 +172,17 @@
         for b in range(blocks):
             c = c_ref[rows(b), cols(h)]
             q = q_ref[rows(b), cols(h)].astype(f32) * jnp.exp(c)
-            qs[h, rows(b)] = pack(q)
+            qs[rows(b), cols(h, 2 * D)] = pack(q)
             qd_ref[rows(b), cols(h, 2 * D)] = pack(q * jnp.exp(before[b]))
-            ks[h, rows(b)] = pack(k_ref[rows(b), cols(h)].astype(f32) * jnp.exp(-c))
-            vs[h, rows(b)] = pack(v_ref[rows(b), cols(h)].astype(f32) * shrink)
-    for h in range(TOGETHER):
-        for b in range(blocks):
-            part = nt(qs[h, rows(b)], ks[h, rows(b)])
-            scores[h, rows(b)] = pack(jnp.where(mask, part, 0.0))
+            ks[rows(b), cols(h, 2 * D)] = pack(k_ref[rows(b), cols(h)].astype(f32) * jnp.exp(-c))
+            vs[rows(b), cols(h, 2 * D)] = pack(v_ref[rows(b), cols(h)].astype(f32) * shrink)
+    for h in range(TOGETHER):
+        for b in range(blocks):
+            part = nt(qs[rows(b), cols(h, 2 * D)], ks[rows(b), cols(h, 2 * D)])
+            scores[rows(b), cols(h, 2 * D)] = pack(jnp.where(mask, part, 0.0))
     for h in range(TOGETHER):
         for b in range(blocks - 1):
-            kv[h, b] = tn(ks[h, rows(b)], vs[h, rows(b)])
+            kv[h, b] = tn(ks[rows(b), cols(h, 2 * D)], vs[rows(b), cols(h, 2 * D)])
     for h in range(TOGETHER):
         key_steps = columns_of(tables[h][1])
         value_step = jnp.exp(-rate_ref[h] * float(BL))
@@ -193,8 +193,8 @@
                 state = (state + kv[h, b]) * (key_steps[:, b : b + 1] * value_step)
     for h in range(TOGETHER):
         for b in range(blocks):
-            value, state = vs[h, rows(b)], pack(starts_ref[h, b])
-            left = jnp.concatenate([scores[h, rows(b)], qs[h, rows(b)]], axis=1)
+            value, state = vs[rows(b), cols(h, 2 * D)], pack(starts_ref[h, b])
+            left = jnp.concatenate([scores[rows(b), cols(h, 2 * D)], qs[rows(b), cols(h, 2 * D)]], axis=1)
             right = jnp.concatenate([value, value, state, state], axis=0)
             core_ref[rows(b), cols(h)] = tables[h][0] * halves(dot(left, right, NN))
 
@@ -274,10 +274,10 @@
 
 
 def block_grad_kernel(
-    blocks, made, q_ref, k_ref, v_ref, c_ref, mid_ref, core_ref, grad_ref, factor_ref,
+    blocks, made, qs, ks, vs, scores, c_ref, mid_ref, core_ref, grad_ref, factor_ref,
     starts_ref, state_ref, rate_ref, gain_ref, *rest,
 ):
-    dq_ref, dk_ref, dv_ref, qs, ks, vs, gs, start, mixed, scores, qg, passed = rest[made:]
+    dq_ref, dk_ref, dv_ref, gs, start, mixed, qg, passed = rest[made:]
     mask = causal()
     tables = []
     for h in range(TOGETHER):
@@ -286,10 +286,6 @@
         key_columns = columns_of(steps + [jnp.exp(x) for x in before])
         tables.append((shrink, key_columns))
         for b in range(blocks):
-            c = c_ref[rows(b), cols(h)]
-            qs[h, rows(b)] = pack(q_ref[rows(b), cols(h)].astype(f32) * jnp.exp(c))
-            ks[h, rows(b)] = pack(k_ref[rows(b), cols(h)].astype(f32) * jnp.exp(-c))
-            vs[h, rows(b)] = pack(v_ref[rows(b), cols(h)].astype(f32) * shrink)
             out = grad_ref[rows(b), cols(h)].astype(f32) * factor_ref[rows(b), :D]
             g = out * gain_ref[h] - core_ref[rows(b), cols(h)] * factor_ref[rows(b), D:]
             gs[h, rows(b)] = pack(g * grow)
@@ -299,13 +295,11 @@
             start[h, rows(b)] = pack(begun)
     for h in range(TOGETHER):
         for b in range(blocks):
-            part = nt(gs[h, rows(b)], vs[h, rows(b)])
+            part = nt(gs[h, rows(b)], vs[rows(b), cols(h, 2 * D)])
             mixed[h, rows(b)] = pack(jnp.where(mask, part, 0.0))
-            part = nt(qs[h, rows(b)], ks[h, rows(b)])
-            scores[h, rows(b)] = pack(jnp.where(mask, part, 0.0))
     for h in range(TOGETHER):
         for b in range(1, blocks):
-            qg[h, b] = tn(qs[h, rows(b)], gs[h, rows(b)])
+            qg[h, b] = tn(qs[rows(b), cols(h, 2 * D)], gs[h, rows(b)])
     for h in range(TOGETHER):
         value_step = jnp.exp(-rate_ref[h] * float(BL))
         now = jnp.zeros((D, D), f32)
@@ -315,15 +309,15 @@
                 now = (now + qg[h, b]) * (tables[h][1][:, b - 1 : b] * value_step)
     for h in range(TOGETHER):
         for b in range(blocks):
-            dq = nn(mixed[h, rows(b)], ks[h, rows(b)]) + nt(gs[h, rows(b)], start[h, rows(b)])
+            dq = nn(mixed[h, rows(b)], ks[rows(b), cols(h, 2 * D)]) + nt(gs[h, rows(b)], start[h, rows(b)])
             dq_ref[rows(b), cols(h)] = (jnp.exp(c_ref[rows(b), cols(h)]) * dq).astype(bf16)
     for h in range(TOGETHER):
         for b in range(blocks):
-            dk = tn(mixed[h, rows(b)], qs[h, rows(b)]) + nt(vs[h, rows(b)], passed[h, rows(b)])
+            dk = tn(mixed[h, rows(b)], qs[rows(b), cols(h, 2 * D)]) + nt(vs[rows(b), cols(h, 2 * D)], passed[h, rows(b)])
             dk_ref[rows(b), cols(h)] = jnp.exp(-c_ref[rows(b), cols(h)]) * dk
     for h in range(TOGETHER):
         for b in range(blocks):
-            dv = tn(scores[h, rows(b)], gs[h, rows(b)]) + nn(ks[h, rows(b)], passed[h, rows(b)])
+            dv = tn(scores[rows(b), cols(h, 2 * D)], gs[h, rows(b)]) + nn(ks[rows(b), cols(h, 2 * D)], passed[h, rows(b)])
             dv_ref[rows(b), cols(h)] = tables[h][0] * dv
 
 
@@ -348,29 +342,31 @@
         gain_out[h] = back_ref[4 * h, 32:33]
 
 
-def forward_scan_kernel(count, pay_ref, out_ref, weight_ref):
-    decays = jnp.concatenate([pay_ref[s, 32:33] for s in range(count)], axis=0)
+def key_weights(count, extra_ref):
+    decays = jnp.concatenate([extra_ref[s, 0:1] for s in range(count)], axis=0)
     padded = jnp.concatenate([decays, jnp.zeros((D - count, D), f32)], axis=0)
-    key_columns = jnp.exp(jnp.transpose(padded)[0:32])
-    value_row = jnp.exp(pay_ref[0, 33:34])
+    return jnp.exp(jnp.transpose(padded)[0:32]), jnp.exp(extra_ref[0, 1:2])
+
+
+def forward_scan_kernel(count, pay_ref, extra_ref, out_ref):
+    key_columns, value_row = key_weights(count, extra_ref)
     state = jnp.zeros((32, D), f32)
     for s in range(count):
         out_ref[s] = state
-        weight = key_columns[:, s : s + 1] * value_row
-        weight_ref[s] = weight
-        state = weight * state + pay_ref[s, 0:32]
-
-
-def backward_scan_kernel(count, scale, pay_ref, weight_ref, out_ref):
+        state = (key_columns[:, s : s + 1] * value_row) * state + pay_ref[s]
+
+
+def backward_scan_kernel(count, scale, pay_ref, gain_ref, extra_ref, out_ref):
+    key_columns, value_row = key_weights(count, extra_ref)
     state = jnp.zeros((32, D), f32)
     gain = jnp.zeros((EXTRA, D), f32)
     for s in range(count):
-        gain = gain + pay_ref[s, 32:40]
+        gain = gain + gain_ref[s]
     gain = gain * scale
     for s in reversed(range(count)):
         out_ref[s, 0:32] = state
         out_ref[s, 32:40] = gain
-        state = weight_ref[s] * state + pay_ref[s, 0:32]
+        state = (key_columns[:, s : s + 1] * value_row) * state + pay_ref[s]
 
 
 def on_device(queries, keys, values, out_grad, log_key_decay, value_rate, norm_gain):
@@ -409,14 +405,16 @@
     wide_low = shape(tokens, width, dtype=bf16)
     pair_shape = shape(tokens, 2 * width, dtype=bf16)
     pay_shape = shape(chunks, 32 + EXTRA, D)
-    params = pltpu.CompilerParams(
-        dimension_semantics=("arbitrary",), vmem_limit_bytes=VMEM_MIB * 1024 * 1024
-    )
-
-    def call(body, name, ins, outs, out_shape, scratch=(), flops=0, steps=turns, aliases={}):
+    def hbm(*arrays):
+        return [pltpu.with_memory_space_constraint(x, pltpu.HBM) for x in arrays]
+
+    def call(body, name, ins, outs, out_shape, scratch=(), flops=0, steps=turns, aliases={}, limit=VMEM_MIB):
         return pl.pallas_call(
             body, name=name, grid=(steps,), in_specs=ins, out_specs=outs, out_shape=out_shape,
-            scratch_shapes=list(scratch), compiler_params=params, input_output_aliases=aliases,
+            scratch_shapes=list(scratch), input_output_aliases=aliases,
+            compiler_params=pltpu.CompilerParams(
+                dimension_semantics=("arbitrary",), vmem_limit_bytes=limit * 1024 * 1024
+            ),
             cost_estimate=pl.CostEstimate(
                 flops=flops, transcendentals=0, bytes_accessed=16 * 1024 * 1024
             ),
@@ -428,26 +426,39 @@
         [pltpu.VMEM((tokens, TOGETHER * D), f32), packed, packed],
     )(keys, values, log_key_decay, rate)
     got = lax.all_to_all(pay, around, 0, 0)
-    local, qd, starts, c, mid = call(
-        functools.partial(local_kernel, blocks), "local",
-        [wide, wide, wide, wide, row], [wide, pair, many, wide, eight],
-        [
-            wide_shape, pair_shape, shape(heads, blocks, D, D), wide_shape,
-            shape(heads, blocks, D),
-        ],
-        [packed, packed, packed, packed, squares], flops=10**10,
-    )(queries, keys, values, log_key_decay, rate)
-    prefixes, weights = pl.pallas_call(
-        functools.partial(forward_scan_kernel, count), name="fscan",
-        out_shape=[shape(chunks, 32, D), shape(chunks, 32, D)],
-    )(got)
+    half = turns // 2
+    made = ()
+    for part in range(2):
+        w, p, r, e, s, m, _ = specs(part * half)
+        made = call(
+            functools.partial(local_kernel, blocks, len(made)), f"local{part}",
+            [w, w, w, w, r] + [pl.BlockSpec(memory_space=pl.ANY)] * len(made),
+            [w, p, m, w, e, p, p, p, p],
+            [
+                wide_shape, pair_shape, shape(heads, blocks, D, D), wide_shape,
+                shape(heads, blocks, D), pair_shape, pair_shape, pair_shape, pair_shape,
+            ],
+            [squares], flops=10**10, steps=half, aliases={5 + i: i for i in range(len(made))},
+        )(queries, keys, values, log_key_decay, rate, *made)
+    local, qd, starts, c, mid, qs, ks, vs, scores = made
+    top = pl.BlockSpec((count, 32, D), lambda i: (0, 0, 0))
+    bottom = pl.BlockSpec((count, EXTRA, D), lambda i: (0, 32 // EXTRA, 0))
+    full = pl.BlockSpec((count, 32 + EXTRA, D), lambda i: (0, 0, 0))
+    small = pltpu.CompilerParams(
+        dimension_semantics=("arbitrary",), vmem_limit_bytes=8 * 1024 * 1024
+    )
+    prefixes = pl.pallas_call(
+        functools.partial(forward_scan_kernel, count), name="fscan", grid=(1,),
+        in_specs=[top, bottom], out_specs=top, out_shape=shape(chunks, 32, D),
+        compiler_params=small,
+    )(got, got)
     state_in = lax.all_to_all(prefixes, around, 0, 0).reshape(heads, D, D)
     core, sums = call(
         functools.partial(core_kernel, blocks, turns), "core",
         [pair, wide, wide, square, row, row], [wide, sums_spec],
-        [wide_shape, shape(head_count, 2 * blocks, D)],
-        [pltpu.VMEM((tokens, D), f32)] * 2,
-    )(qd, local, out_grad, state_in, rate, gain)
+        [pltpu.HBM(wide_shape.shape, f32), shape(head_count, 2 * blocks, D)],
+        [pltpu.VMEM((tokens, D), f32)] * 2, limit=24,
+    )(*hbm(qd, local, out_grad), state_in, rate, gain)
     all_sums = lax.all_to_all(sums, "head", 0, 0)
     back_pay, factor = call(
         functools.partial(grad_kernel, blocks), "grad",
@@ -455,32 +466,33 @@
         [pay_shape, shape(tokens, 2 * D)], [packed],
     )(qd, core, out_grad, all_sums, rate, gain)
     back_got = lax.all_to_all(back_pay, around, 0, 0)
-    half = turns // 2
     made = ()
     for part in range(2):
-        w, _, r, e, s, m, _ = specs(part * half)
+        w, p, r, e, s, m, _ = specs(part * half)
         made = call(
             functools.partial(block_grad_kernel, blocks, len(made)), f"blockgrad{part}",
-            [w, w, w, w, e, w, w, factors, m, s, r, r]
+            [p, p, p, p, w, e, w, w, factors, m, s, r, r]
             + [pl.BlockSpec(memory_space=pl.ANY)] * len(made),
             [w, w, w], [wide_low, wide_shape, wide_shape],
-            [packed] * 7 + [squares, packed], flops=10**10, steps=half,
-            aliases={12 + i: i for i in range(len(made))},
+            [packed] * 3 + [squares, packed], flops=10**10, steps=half,
+            aliases={13 + i: i for i in range(len(made))},
         )(
-            queries, keys, values, c, mid, core, out_grad, factor, starts, state_in, rate, gain,
+            qs, ks, vs, scores, c, mid, core, out_grad, factor, starts, state_in, rate, gain,
             *made,
         )
     dq, dk_local, dv_local = made
     scale = 1.0 / math.sqrt(tokens * count)
     back_prefixes = pl.pallas_call(
-        functools.partial(backward_scan_kernel, count, scale), name="bscan", out_shape=pay_shape,
-    )(back_got, weights)
+        functools.partial(backward_scan_kernel, count, scale), name="bscan", grid=(1,),
+        in_specs=[top, bottom, bottom], out_specs=full, out_shape=pay_shape,
+        compiler_params=small,
+    )(back_got, back_got, got)
     back_in = lax.all_to_all(back_prefixes, around, 0, 0)
     dk, dv, gain_grad = call(
         functools.partial(final_kernel, blocks), "final",
         [wide, wide, wide, eight, wide, wide, payload, row], [wide, wide, row],
-        [wide_low, wide_low, shape(heads, 1, D)],
-    )(keys, values, c, mid, dk_local, dv_local, back_in, rate)
+        [wide_low, wide_low, shape(heads, 1, D)], limit=24,
+    )(*hbm(keys, values, c), mid, *hbm(dk_local, dv_local), back_in, rate)
     return dq, dk, dv, gain_grad.reshape(width)
 
 

time: 133 us -> 122 us (0.917)
  blocking collectives: 30.3 us -> 8.2 us
  starting transfers between devices: 21 us -> 29.3 us
  waiting for transfers between devices: 0.01 us -> 4.16 us
  local copies, waits for them, and re-layouts: 2.46 us -> 0.03 us
  Pallas kernels: 77.2 us -> 78.8 us
    all_to_all x1 -> x0, blocking collectives: 21.9 us -> none  [on_device(): got = lax.all_to_all(pay, around, 0, 0)]
    all_to_all x0 -> x1, starting transfers between devices: none -> 9.6 us  [on_device(): got = lax.all_to_all(pay, around, 0, 0)]
    pallas_call x1 -> x2, Pallas kernels: 13.3 us -> 19.3 us  [on_device(): call(functools.partial(local_kernel, blocks, len(made)), f'local{part}',...]
    all_to_all x0 -> x1, waiting for transfers between devices: none -> 2.52 us  [on_device(): got = lax.all_to_all(pay, around, 0, 0)]
    unnamed x6 -> x10, local copies, waits for them, and re-layouts: 2.46 us -> 0.03 us
    pallas_call x2, Pallas kernels: 27.3 us -> 25.1 us  [on_device(): call(functools.partial(block_grad_kernel, blocks, len(made)), f'blockgrad...]
    all_to_all x1, starting transfers between devices: 8.88 us -> 7.42 us  [on_device(): back_got = lax.all_to_all(back_pay, around, 0, 0)]
    all_to_all x1, waiting for transfers between devices: 0.01 us -> 1.38 us  [on_device(): state_in = lax.all_to_all(prefixes, around, 0, 0).reshape(heads, D, D)]
  transfers between devices with their start and end apart: 3 -> 4, of which waited for: 0 -> 3; matrix products, arithmetic and copies ran while one was open for 0% -> 0% of each run, Pallas kernels for 31% -> 37%
where the time goes in v1:
time: 122 us; the launch traced here: 121 us
  Pallas kernels  78.8 us (65%)
  starting transfers between devices  29.3 us (24%)
  blocking collectives  8.2 us (7%)
  waiting for transfers between devices  4.16 us (3%)
    pallas_call x2, Pallas kernels, on_device(): call(functools.partial(block_grad_kernel, blocks, len(made)), f'blockgrad...  25.1 us
    pallas_call x2, Pallas kernels, on_device(): call(functools.partial(local_kernel, blocks, len(made)), f'local{part}',...  19.3 us
    pallas_call x1, Pallas kernels, on_device(): call(functools.partial(final_kernel, blocks), 'final', [wide, wide, wide,...  9.65 us
    all_to_all x1, starting transfers between devices, on_device(): got = lax.all_to_all(pay, around, 0, 0)  9.6 us
    all_to_all x1, blocking collectives, on_device(): all_sums = lax.all_to_all(sums, 'head', 0, 0)  8.2 us
    pallas_call x1, Pallas kernels, on_device(): call(functools.partial(core_kernel, blocks, turns), 'core', [pair, wide,...  7.83 us
    all_to_all x1, starting transfers between devices, on_device(): back_got = lax.all_to_all(back_pay, around, 0, 0)  7.42 us
    all_to_all x1, starting transfers between devices, on_device(): back_in = lax.all_to_all(back_prefixes, around, 0, 0)  7.37 us
  transfers between devices with their start and end apart: 4, of which 3 were waited for; matrix products, arithmetic and copies ran while one was open for 0% of the time, Pallas kernels for 37%

profile of v1, /device:TPU:1, one launch (start us, length us, event | category | flops | bytes accessed | tf_op | source)
XLA Modules:
  0.0 121.2 jit_solution(3330531583717569823)
XLA Ops:
  0.6 7.2 %state.1 = f32[32,40,128]{2,1,0:T(8,128)} custom-call(bf16[1024,1024]{1,0:T(8,128)(2,1)} %k_ref.7, bf16[1024,1024]{1,0:T(8,128)(2,1)} %v_ref.7, f32[1024,1024]{1,0:T(8,128)} %ld_ref.5, f32[8,1,128]{2,1,0:T(1,128)} %bitcast.7), custom_call_target="tpu_custom_call" | custom-call | bytes 16777216 | tf_op jit(solution)/shard_map/state/pallas_call | solution.py:423
  7.8 9.6 %all-to-all-start = ((f32[32,40,128]{2,1,0:T(8,128)}), f32[32,40,128]{2,1,0:T(8,128)S(1)}, u32[]{:S(2)}, u32[]{:S(2)}) async-start(f32[32,40,128]{2,1,0:T(8,128)} %state.1), calls=%async_computation | async-start | bytes 1310720 | tf_op jit(solution)/shard_map/all_to_all | solution.py:428
  17.4 9.7 %local0.1 = (f32[1024,1024]{1,0:T(8,128)}, bf16[1024,2048]{1,0:T(8,128)(2,1)}, f32[8,8,128,128]{3,2,1,0:T(8,128)}, f32[1024,1024]{1,0:T(8,128)}, f32[8,8,128]{2,...) custom-call(bf16[1024,1024]{1,0:T(8,128)(2,1)} %q_ref.3, ...), custom_call_target="tpu_custom_call" | custom-call | flops 10000000000 | bytes 16777216 | tf_op jit(solution)/shard_map/local0/pallas_call | solution.py:433
  27.1 2.5 %all-to-all-done.pay_ref.extra_ref = f32[32,40,128]{2,1,0:T(8,128)S(1)} async-done(((f32[32,40,128]{2,1,0:T(8,128)}), f32[32,40,128]{2,1,0:T(8,128)S(1)}, u32[]{:S(2)}, u32[]{:S(2)}) %all-to-all-start) | async-done | bytes 655392 | tf_op jit(solution)/shard_map/all_to_all | solution.py:428
  29.6 1.2 fscan.1
  30.7 4.9 %all-to-all-start.1 = ((f32[32,32,128]{2,1,0:T(8,128)}), f32[32,32,128]{2,1,0:T(8,128)S(1)}, u32[]{:S(2)}, u32[]{:S(2)}) async-start(f32[32,32,128]{2,1,0:T(8,128)} %fscan.1), calls=%async_computation.1 | async-start | bytes 1048576 | tf_op jit(solution)/shard_map/all_to_all | solution.py:455
  35.6 0.0 copy-start.2
  35.6 0.0 copy-start.4
  35.6 9.7 %local1.1 = (f32[1024,1024]{1,0:T(8,128)}, bf16[1024,2048]{1,0:T(8,128)(2,1)}, f32[8,8,128,128]{3,2,1,0:T(8,128)}, f32[1024,1024]{1,0:T(8,128)}, f32[8,8,128]{2,...) custom-call(bf16[1024,1024]{1,0:T(8,128)(2,1)} %q_ref.3, ...), custom_call_target="tpu_custom_call", output_to_operand_aliasing={{0}: (5, {}), {1}: (6, {}), {2}: (7, {}), {3}: (8, {}), {4}... | custom-call | flops 10000000000 | bytes 16777216 | tf_op jit(solution)/shard_map/local1/pallas_call | solution.py:433
  45.3 1.4 %all-to-all-done.1 = f32[32,32,128]{2,1,0:T(8,128)S(1)} async-done(((f32[32,32,128]{2,1,0:T(8,128)}), f32[32,32,128]{2,1,0:T(8,128)S(1)}, u32[]{:S(2)}, u32[]{:S(2)}) %all-to-all-start.1) | async-done | bytes 524320 | tf_op jit(solution)/shard_map/all_to_all | solution.py:455
  46.7 0.0 copy-start
  46.7 0.0 copy-done.2
  46.7 0.0 copy-done.4
  46.7 7.8 %core.1 = (f32[1024,1024]{1,0:T(8,128)}, f32[4,16,128]{2,1,0:T(8,128)S(1)}) custom-call(bf16[1024,2048]{1,0:T(8,128)(2,1)} %get-tuple-element.50.qd_ref, f32[1024,1024]{1,0:T(8,128)} %get-tuple-element.51.local_ref, bf16[1024,1024]{1,0:T(8,128)(2,1)} %grad_ref.7, f32[8,128,128]{2,1,0:T(8,128)S(1)} %bitcast.4, f32[8,1,128]{2,1,0:T(1,128)S(1)} %bitcast.13, ...), custom_call_target="tpu_custom_call" | custom-call | bytes 16777216 | tf_op jit(solution)/shard_map/core/pallas_call | solution.py:456
  54.5 0.0 copy-done
  54.5 8.2 %all_to_all.25.sums_ref = f32[4,16,128]{2,1,0:T(8,128)} all-to-all(f32[4,16,128]{2,1,0:T(8,128)S(1)} %get-tuple-element.53), channel_id=1, replica_groups=mesh['outer'=8,'inner'=4,'head'=4] {'head'}, dimensions={0} | all-to-all | bytes 65536 | tf_op jit(solution)/shard_map/all_to_all | solution.py:462
  62.7 7.3 %grad.1 = (f32[32,40,128]{2,1,0:T(8,128)}, f32[1024,256]{1,0:T(8,128)}) custom-call(bf16[1024,2048]{1,0:T(8,128)(2,1)} %get-tuple-element.50.qd_ref, f32[1024,1024]{1,0:T(8,128)} %get-tuple-element.52.core_ref, bf16[1024,1024]{1,0:T(8,128)(2,1)} %grad_ref.7, f32[4,16,128]{2,1,0:T(8,128)} %all_to_all.25.sums_ref, f32[8,1,128]{2,1,0:T(1,128)} %bitcast.10, ...), custom_call_target="tpu_custom_call" | custom-call | bytes 16777216 | tf_op jit(solution)/shard_map/grad/pallas_call | solution.py:463
  70.1 7.4 %all-to-all-start.3 = ((f32[32,40,128]{2,1,0:T(8,128)}), f32[32,40,128]{2,1,0:T(8,128)S(1)}, u32[]{:S(2)}, u32[]{:S(2)}) async-start(f32[32,40,128]{2,1,0:T(8,128)} %get-tuple-element.62), calls=%async_computation.3 | async-start | bytes 1310720 | tf_op jit(solution)/shard_map/all_to_all | solution.py:468
  77.5 13.2 %blockgrad0.1 = (bf16[1024,1024]{1,0:T(8,128)(2,1)}, f32[1024,1024]{1,0:T(8,128)}, f32[1024,1024]{1,0:T(8,128)}) custom-call(bf16[1024,2048]{1,0:T(8,128)(2,1)} %get-tuple-element.44.qs, bf16[1024,2048]{1,0:T(8,128)(2,1)} %get-tuple-element.45.ks, bf16[1024,2048]{1,0:T(8,128)(2,1)} %get-tuple-element.46.vs, bf16[1024,2048]{1,0:T(8,128)(2,1)} %get-tuple-element.47.scores, ...), custom_call_target="tpu_custom_call" | custom-call | flops 10000000000 | bytes 16777216 | tf_op jit(solution)/shard_map/blockgrad0/pallas_call | solution.py:472
  90.7 0.0 all-to-all-done.3.pay_ref.gain_ref
  90.7 1.2 bscan.1
  91.9 7.4 %all-to-all-start.4 = ((f32[32,40,128]{2,1,0:T(8,128)}), f32[32,40,128]{2,1,0:T(8,128)S(1)}, u32[]{:S(2)}, u32[]{:S(2)}) async-start(f32[32,40,128]{2,1,0:T(8,128)} %bscan.1), calls=%async_computation.4 | async-start | bytes 1310720 | tf_op jit(solution)/shard_map/all_to_all | solution.py:490
  99.3 0.0 copy-start.1
  99.3 0.0 copy-start.3
  99.3 11.9 %blockgrad1.1 = (bf16[1024,1024]{1,0:T(8,128)(2,1)}, f32[1024,1024]{1,0:T(8,128)}, f32[1024,1024]{1,0:T(8,128)}) custom-call(bf16[1024,2048]{1,0:T(8,128)(2,1)} %get-tuple-element.44.qs, bf16[1024,2048]{1,0:T(8,128)(2,1)} %get-tuple-element.45.ks, ...), custom_call_target="tpu_custom_call", output_to_operand_aliasing={{0}: (13, {}), {1}: (14, {}), {2}: (15, {})} | custom-call | flops 10000000000 | bytes 16777216 | tf_op jit(solution)/shard_map/blockgrad1/pallas_call | solution.py:472
  111.2 0.3 all-to-all-done.4.back_ref
  111.5 0.0 copy-done.1
  111.5 0.0 copy-done.3
  111.5 9.7 %final.1 = (bf16[1024,1024]{1,0:T(8,128)(2,1)}, bf16[1024,1024]{1,0:T(8,128)(2,1)}, f32[8,1,128]{2,1,0:T(1,128)}) custom-call(bf16[1024,1024]{1,0:T(8,128)(2,1)} %k_ref.7, bf16[1024,1024]{1,0:T(8,128)(2,1)} %v_ref.7, f32[1024,1024]{1,0:T(8,128)} %get-tuple-element.48.c_ref, f32[8,8,128]{2,1,0:T(8,128)S(1)} %copy-done.1, ...), custom_call_target="tpu_custom_call" | custom-call | bytes 16777216 | tf_op jit(solution)/shard_map/final/pallas_call | solution.py:491
Async XLA Ops:
  7.8 21.8 %all-to-all-start = ((f32[32,40,128]{2,1,0:T(8,128)}), f32[32,40,128]{2,1,0:T(8,128)S(1)}, u32[]{:S(2)}, u32[]{:S(2)}) async-start(f32[32,40,128]{2,1,0:T(8,128)} %state.1), calls=%async_computation | async-start | bytes 1310720 | tf_op jit(solution)/shard_map/all_to_all | solution.py:428
  30.7 16.0 %all-to-all-start.1 = ((f32[32,32,128]{2,1,0:T(8,128)}), f32[32,32,128]{2,1,0:T(8,128)S(1)}, u32[]{:S(2)}, u32[]{:S(2)}) async-start(f32[32,32,128]{2,1,0:T(8,128)} %fscan.1), calls=%async_computation.1 | async-start | bytes 1048576 | tf_op jit(solution)/shard_map/all_to_all | solution.py:455
  35.6 11.1 %copy-start.2 = (f32[1024]{0:T(1024)S(1)}, f32[1024]{0:T(1024)}, u32[]{:S(2)}) copy-start(f32[1024]{0:T(1024)} %param.12) | copy-start | bytes 12292
  35.6 11.1 %copy-start.4 = (f32[1024]{0:T(1024)S(1)}, f32[1024]{0:T(1024)}, u32[]{:S(2)}) copy-start(f32[1024]{0:T(1024)} %param.13) | copy-start | bytes 12292
  46.7 7.8 %copy-start = (f32[32,32,128]{2,1,0:T(8,128)}, f32[32,32,128]{2,1,0:T(8,128)S(1)}, u32[]{:S(2)}) copy-start(f32[32,32,128]{2,1,0:T(8,128)S(1)} %all-to-all-done.1) | copy-start | bytes 1572868
  70.1 20.7 %all-to-all-start.3 = ((f32[32,40,128]{2,1,0:T(8,128)}), f32[32,40,128]{2,1,0:T(8,128)S(1)}, u32[]{:S(2)}, u32[]{:S(2)}) async-start(f32[32,40,128]{2,1,0:T(8,128)} %get-tuple-element.62), calls=%async_computation.3 | async-start | bytes 1310720 | tf_op jit(solution)/shard_map/all_to_all | solution.py:468
  91.9 19.6 %all-to-all-start.4 = ((f32[32,40,128]{2,1,0:T(8,128)}), f32[32,40,128]{2,1,0:T(8,128)S(1)}, u32[]{:S(2)}, u32[]{:S(2)}) async-start(f32[32,40,128]{2,1,0:T(8,128)} %bscan.1), calls=%async_computation.4 | async-start | bytes 1310720 | tf_op jit(solution)/shard_map/all_to_all | solution.py:490
  99.3 12.2 %copy-start.1 = (f32[8,8,128]{2,1,0:T(8,128)S(1)}, f32[8,8,128]{2,1,0:T(8,128)}, u32[]{:S(2)}) copy-start(f32[8,8,128]{2,1,0:T(8,128)} %get-tuple-element.49.mid_ref) | copy-start | bytes 98308
  99.3 12.2 %copy-start.3 = (f32[1024]{0:T(1024)S(1)}, f32[1024]{0:T(1024)}, u32[]{:S(2)}) copy-start(f32[1024]{0:T(1024)} %param.12) | copy-start | bytes 12292

commit v2 on v1

--- a/solution.py
+++ b/solution.py
@@ -201,9 +201,11 @@
 
 def core_kernel(
     blocks, turns, qd_ref, local_ref, grad_ref, state_ref, rate_ref, gain_ref,
-    core_ref, sums_ref, squares, crosses,
+    near_ref, near_qd_ref, near_grad_ref, sums_ref, squares, crosses,
 ):
     turn = pl.program_id(0)
+    near_qd_ref[...] = qd_ref[...]
+    near_grad_ref[...] = grad_ref[...]
 
     @pl.when(turn == 0)
     def _():
@@ -221,7 +223,7 @@
             reach = jnp.exp(-rate_ref[h] * float(BL * b + HALF))
             incoming = halves(dot(qd_ref[rows(b), cols(h, 2 * D)], rights[h], NN))
             core = local_ref[rows(b), cols(h)] + (grows[h] * reach) * incoming
-            core_ref[rows(b), cols(h)] = core
+            near_ref[rows(b), cols(h)] = core
             square = square + core * core
             cross = cross + core * (grad_ref[rows(b), cols(h)].astype(f32) * gain_ref[h])
         squares[rows(b)] = square
@@ -238,16 +240,17 @@
 
 
 def grad_kernel(
-    blocks, qd_ref, core_ref, grad_ref, sums_ref, rate_ref, gain_ref, pay_ref, factor_ref, gg
+    blocks, qd_ref, core_ref, grad_ref, rate_ref, gain_ref, *rest
 ):
+    *sums_refs, pay_ref, factor_ref, kept_ref, gg = rest
     turn = pl.program_id(0)
     columns = HEADS * D
 
     @pl.when(turn == 0)
     def _():
-        both = sums_ref[0]
-        for copy in range(1, sums_ref.shape[0]):
-            both = both + sums_ref[copy]
+        both = sums_refs[0][0]
+        for ref in sums_refs[1:]:
+            both = both + ref[0]
         rms = lax.rsqrt(both[0:blocks] / columns + 1e-06)
         coef = rms * rms * rms * both[blocks : 2 * blocks] / columns
         for b in range(blocks):
@@ -259,6 +262,7 @@
         gain_sum = jnp.zeros((BL, D), f32)
         for b in range(blocks):
             core = core_ref[rows(b), cols(h)]
+            kept_ref[rows(b), cols(h)] = core
             out = grad_ref[rows(b), cols(h)].astype(f32) * factor_ref[rows(b), :D]
             gain_sum = gain_sum + out * core
             g = out * gain_ref[h] - core * factor_ref[rows(b), D:]
@@ -396,7 +400,7 @@
     factors = pl.BlockSpec((tokens, 2 * D), lambda h: (0, 0))
     packed = pltpu.VMEM((TOGETHER, tokens, 2 * D), bf16)
     squares = pltpu.VMEM((TOGETHER, blocks, D, D), f32)
-    sums_spec = pl.BlockSpec((head_count, 2 * blocks, D), lambda h: (0, 0, 0))
+    sums_spec = pl.BlockSpec((1, 2 * blocks, D), lambda h: (0, 0, 0))
 
     def shape(*dims, dtype=f32):
         return jax.ShapeDtypeStruct(dims, dtype)
@@ -453,18 +457,24 @@
         compiler_params=small,
     )(got, got)
     state_in = lax.all_to_all(prefixes, around, 0, 0).reshape(heads, D, D)
-    core, sums = call(
+    near, near_qd, near_grad, sums = call(
         functools.partial(core_kernel, blocks, turns), "core",
-        [pair, wide, wide, square, row, row], [wide, sums_spec],
-        [pltpu.HBM(wide_shape.shape, f32), shape(head_count, 2 * blocks, D)],
+        [pair, wide, wide, square, row, row], [wide, pair, wide, sums_spec],
+        [
+            wide_shape, pair_shape, wide_low, shape(1, 2 * blocks, D),
+        ],
         [pltpu.VMEM((tokens, D), f32)] * 2, limit=24,
     )(*hbm(qd, local, out_grad), state_in, rate, gain)
-    all_sums = lax.all_to_all(sums, "head", 0, 0)
-    back_pay, factor = call(
+    all_sums = [sums] + [
+        lax.ppermute(sums, "head", [(i, i ^ step) for i in range(head_count)])
+        for step in (2, 1, 3)
+    ]
+    back_pay, factor, core = call(
         functools.partial(grad_kernel, blocks), "grad",
-        [pair, wide, wide, sums_spec, row, row], [payload, factors],
-        [pay_shape, shape(tokens, 2 * D)], [packed],
-    )(qd, core, out_grad, all_sums, rate, gain)
+        [pair, wide, wide, row, row] + [sums_spec] * head_count, [payload, factors, wide],
+        [pay_shape, pltpu.HBM((tokens, 2 * D), f32), pltpu.HBM(wide_shape.shape, f32)],
+        [packed], limit=24,
+    )(near_qd, near, near_grad, rate, gain, *all_sums)
     back_got = lax.all_to_all(back_pay, around, 0, 0)
     made = ()
     for part in range(2):

time: 122 us -> 118 us (0.967)
  blocking collectives: 8.2 us -> 0 us
  starting transfers between devices: 29.3 us -> 33.1 us
  waiting for transfers between devices: 4.16 us -> 7.45 us
  Pallas kernels: 78.8 us -> 75.9 us
    all_to_all x1 -> x0, blocking collectives: 8.2 us -> none  [on_device(): all_sums = lax.all_to_all(sums, 'head', 0, 0)]
    ppermute x0 -> x3, starting transfers between devices: none -> 3.68 us  [on_device(): lax.ppermute(sums, 'head', [(i, i ^ step) for i in range(head_count)])]
    ppermute x0 -> x3, waiting for transfers between devices: none -> 3.15 us  [on_device(): lax.ppermute(sums, 'head', [(i, i ^ step) for i in range(head_count)])]
    pallas_call x1, Pallas kernels: 7.33 us -> 5.49 us  [on_device(): call(functools.partial(grad_kernel, blocks), 'grad', [pair, wide, wide, r...]
  transfers between devices with their start and end apart: 4 -> 7, of which waited for: 3 -> 6; matrix products, arithmetic and copies ran while one was open for 0% -> 0% of each run, Pallas kernels for 37% -> 38%
where the time goes in v2:
time: 118 us; the launch traced here: 117 us
  Pallas kernels  75.9 us (64%)
  starting transfers between devices  33.1 us (28%)
  waiting for transfers between devices  7.45 us (6%)
    pallas_call x2, Pallas kernels, on_device(): call(functools.partial(block_grad_kernel, blocks, len(made)), f'blockgrad...  25.1 us
    pallas_call x2, Pallas kernels, on_device(): call(functools.partial(local_kernel, blocks, len(made)), f'local{part}',...  19.2 us
    pallas_call x1, Pallas kernels, on_device(): call(functools.partial(final_kernel, blocks), 'final', [wide, wide, wide,...  9.65 us
    all_to_all x1, starting transfers between devices, on_device(): got = lax.all_to_all(pay, around, 0, 0)  9.6 us
    all_to_all x1, starting transfers between devices, on_device(): back_got = lax.all_to_all(back_pay, around, 0, 0)  7.62 us
    all_to_all x1, starting transfers between devices, on_device(): back_in = lax.all_to_all(back_prefixes, around, 0, 0)  7.37 us
    pallas_call x1, Pallas kernels, on_device(): call(functools.partial(state_kernel, blocks), 'state', [wide, wide, wide,...  7.16 us
    pallas_call x1, Pallas kernels, on_device(): call(functools.partial(core_kernel, blocks, turns), 'core', [pair, wide,...  6.93 us
  transfers between devices with their start and end apart: 7, of which 6 were waited for; matrix products, arithmetic and copies ran while one was open for 0% of the time, Pallas kernels for 38%

profile of v2, /device:TPU:1, one launch (start us, length us, event | category | flops | bytes accessed | tf_op | source)
XLA Modules:
  0.0 117.2 jit_solution(7291725030826699698)
XLA Ops:
  0.6 7.2 %state.1 = f32[32,40,128]{2,1,0:T(8,128)} custom-call(bf16[1024,1024]{1,0:T(8,128)(2,1)} %k_ref.7, bf16[1024,1024]{1,0:T(8,128)(2,1)} %v_ref.7, f32[1024,1024]{1,0:T(8,128)} %ld_ref.5, f32[8,1,128]{2,1,0:T(1,128)} %bitcast.7), custom_call_target="tpu_custom_call" | custom-call | bytes 16777216 | tf_op jit(solution)/shard_map/state/pallas_call | solution.py:427
  7.8 9.6 %all-to-all-start = ((f32[32,40,128]{2,1,0:T(8,128)}), f32[32,40,128]{2,1,0:T(8,128)S(1)}, u32[]{:S(2)}, u32[]{:S(2)}) async-start(f32[32,40,128]{2,1,0:T(8,128)} %state.1), calls=%async_computation | async-start | bytes 1310720 | tf_op jit(solution)/shard_map/all_to_all | solution.py:432
  17.4 9.6 %local0.1 = (f32[1024,1024]{1,0:T(8,128)}, bf16[1024,2048]{1,0:T(8,128)(2,1)}, f32[8,8,128,128]{3,2,1,0:T(8,128)}, f32[1024,1024]{1,0:T(8,128)}, f32[8,8,128]{2,...) custom-call(bf16[1024,1024]{1,0:T(8,128)(2,1)} %q_ref.3, ...), custom_call_target="tpu_custom_call" | custom-call | flops 10000000000 | bytes 16777216 | tf_op jit(solution)/shard_map/local0/pallas_call | solution.py:437
  27.0 2.6 %all-to-all-done.pay_ref.extra_ref = f32[32,40,128]{2,1,0:T(8,128)S(1)} async-done(((f32[32,40,128]{2,1,0:T(8,128)}), f32[32,40,128]{2,1,0:T(8,128)S(1)}, u32[]{:S(2)}, u32[]{:S(2)}) %all-to-all-start) | async-done | bytes 655392 | tf_op jit(solution)/shard_map/all_to_all | solution.py:432
  29.6 1.2 fscan.1
  30.7 4.8 %all-to-all-start.1 = ((f32[32,32,128]{2,1,0:T(8,128)}), f32[32,32,128]{2,1,0:T(8,128)S(1)}, u32[]{:S(2)}, u32[]{:S(2)}) async-start(f32[32,32,128]{2,1,0:T(8,128)} %fscan.1), calls=%async_computation.1 | async-start | bytes 1048576 | tf_op jit(solution)/shard_map/all_to_all | solution.py:459
  35.5 0.0 copy-start.2
  35.5 0.0 copy-start.4
  35.6 9.6 %local1.1 = (f32[1024,1024]{1,0:T(8,128)}, bf16[1024,2048]{1,0:T(8,128)(2,1)}, f32[8,8,128,128]{3,2,1,0:T(8,128)}, f32[1024,1024]{1,0:T(8,128)}, f32[8,8,128]{2,...) custom-call(bf16[1024,1024]{1,0:T(8,128)(2,1)} %q_ref.3, ...), custom_call_target="tpu_custom_call", output_to_operand_aliasing={{0}: (5, {}), {1}: (6, {}), {2}: (7, {}), {3}: (8, {}), {4}... | custom-call | flops 10000000000 | bytes 16777216 | tf_op jit(solution)/shard_map/local1/pallas_call | solution.py:437
  45.2 1.5 %all-to-all-done.1 = f32[32,32,128]{2,1,0:T(8,128)S(1)} async-done(((f32[32,32,128]{2,1,0:T(8,128)}), f32[32,32,128]{2,1,0:T(8,128)S(1)}, u32[]{:S(2)}, u32[]{:S(2)}) %all-to-all-start.1) | async-done | bytes 524320 | tf_op jit(solution)/shard_map/all_to_all | solution.py:459
  46.6 0.0 copy-start
  46.6 0.0 copy-done.2
  46.6 0.0 copy-done.4
  46.6 6.9 %core.1 = (f32[1024,1024]{1,0:T(8,128)S(1)}, bf16[1024,2048]{1,0:T(8,128)(2,1)S(1)}, bf16[1024,1024]{1,0:T(8,128)(2,1)S(1)}, f32[1,16,128]{2,1,0:T(8,128)S(1)}) custom-call(bf16[1024,2048]{1,0:T(8,128)(2,1)} %get-tuple-element.53.qd_ref, f32[1024,1024]{1,0:T(8,128)} %get-tuple-element.54.local_ref, bf16[1024,1024]{1,0:T(8,128)(2,1)} %grad_ref.5, ...), custom_call_target="tpu_custom_call" | custom-call | bytes 16777216 | tf_op jit(solution)/shard_map/core/pallas_call | solution.py:460
  53.6 0.0 copy-done
  53.6 2.8 %collective-permute-start = (f32[1,16,128]{2,1,0:T(8,128)S(1)}, f32[1,16,128]{2,1,0:T(8,128)S(1)}, u32[]{:S(2)}, u32[]{:S(2)}) collective-permute-start(f32[1,16,128]{2,1,0:T(8,128)S(1)} %get-tuple-element.58.rest_0_), channel_id=1, source_target_pairs={{0,2},{1,3},{2,0},{3,1},{4,6},{5,7},{6,4},{7,5},{8,10},{9,11},{10,... | collective-permute-start | bytes 24584 | tf_op jit(solution)/shard_map/ppermute | solution.py:469
  56.4 0.3 collective-permute-start.1
  56.7 0.6 collective-permute-start.2
  57.3 0.4 collective-permute-done.rest_1_
  57.7 1.5 %collective-permute-done.1.rest_2_ = f32[1,16,128]{2,1,0:T(8,128)S(1)} collective-permute-done((f32[1,16,128]{2,1,0:T(8,128)S(1)}, f32[1,16,128]{2,1,0:T(8,128)S(1)}, u32[]{:S(2)}, u32[]{:S(2)}) %collective-permute-start.1) | collective-permute-done | bytes 8224 | tf_op jit(solution)/shard_map/ppermute | solution.py:469
  59.2 1.2 %collective-permute-done.2.rest_3_ = f32[1,16,128]{2,1,0:T(8,128)S(1)} collective-permute-done((f32[1,16,128]{2,1,0:T(8,128)S(1)}, f32[1,16,128]{2,1,0:T(8,128)S(1)}, u32[]{:S(2)}, u32[]{:S(2)}) %collective-permute-start.2) | collective-permute-done | bytes 8224 | tf_op jit(solution)/shard_map/ppermute | solution.py:469
  60.4 5.5 %grad.1 = (f32[32,40,128]{2,1,0:T(8,128)}, f32[1024,256]{1,0:T(8,128)}, f32[1024,1024]{1,0:T(8,128)}) custom-call(bf16[1024,2048]{1,0:T(8,128)(2,1)S(1)} %get-tuple-element.55.qd_ref, f32[1024,1024]{1,0:T(8,128)S(1)} %get-tuple-element.56.core_ref, bf16[1024,1024]{1,0:T(8,128)(2,1)S(1)} %get-tuple-element.57.grad_ref, f32[8,1,128]{2,1,0:T(1,128)S(1)} %bitcast.13, ...), custom_call_target="tpu_custom_call" | custom-call | bytes 16777216 | tf_op jit(solution)/shard_map/grad/pallas_call | solution.py:472
  65.9 7.6 %all-to-all-start.2 = ((f32[32,40,128]{2,1,0:T(8,128)}), f32[32,40,128]{2,1,0:T(8,128)S(1)}, u32[]{:S(2)}, u32[]{:S(2)}) async-start(f32[32,40,128]{2,1,0:T(8,128)} %get-tuple-element.68), calls=%async_computation.2 | async-start | bytes 1310720 | tf_op jit(solution)/shard_map/all_to_all | solution.py:478
  73.6 13.2 %blockgrad0.1 = (bf16[1024,1024]{1,0:T(8,128)(2,1)}, f32[1024,1024]{1,0:T(8,128)}, f32[1024,1024]{1,0:T(8,128)}) custom-call(bf16[1024,2048]{1,0:T(8,128)(2,1)} %get-tuple-element.47.qs, bf16[1024,2048]{1,0:T(8,128)(2,1)} %get-tuple-element.48.ks, bf16[1024,2048]{1,0:T(8,128)(2,1)} %get-tuple-element.49.vs, bf16[1024,2048]{1,0:T(8,128)(2,1)} %get-tuple-element.50.scores, ...), custom_call_target="tpu_custom_call" | custom-call | flops 10000000000 | bytes 16777216 | tf_op jit(solution)/shard_map/blockgrad0/pallas_call | solution.py:482
  86.8 0.0 all-to-all-done.2.pay_ref.gain_ref
  86.8 1.2 %bscan.1 = f32[32,40,128]{2,1,0:T(8,128)} custom-call(f32[32,40,128]{2,1,0:T(8,128)S(1)} %all-to-all-done.2.pay_ref.gain_ref, f32[32,40,128]{2,1,0:T(8,128)S(1)} %all-to-all-done.2.pay_ref.gain_ref, f32[32,40,128]{2,1,0:T(8,128)S(1)} %all-to-all-done.pay_ref.extra_ref), custom_call_target="tpu_custom_call" | custom-call | tf_op jit(solution)/shard_map/bscan/pallas_call | solution.py:495
  88.0 7.4 %all-to-all-start.3 = ((f32[32,40,128]{2,1,0:T(8,128)}), f32[32,40,128]{2,1,0:T(8,128)S(1)}, u32[]{:S(2)}, u32[]{:S(2)}) async-start(f32[32,40,128]{2,1,0:T(8,128)} %bscan.1), calls=%async_computation.3 | async-start | bytes 1310720 | tf_op jit(solution)/shard_map/all_to_all | solution.py:500
  95.4 0.0 copy-start.1
  95.4 0.0 copy-start.3
  95.4 11.9 %blockgrad1.1 = (bf16[1024,1024]{1,0:T(8,128)(2,1)}, f32[1024,1024]{1,0:T(8,128)}, f32[1024,1024]{1,0:T(8,128)}) custom-call(bf16[1024,2048]{1,0:T(8,128)(2,1)} %get-tuple-element.47.qs, bf16[1024,2048]{1,0:T(8,128)(2,1)} %get-tuple-element.48.ks, ...), custom_call_target="tpu_custom_call", output_to_operand_aliasing={{0}: (13, {}), {1}: (14, {}), {2}: (15, {})} | custom-call | flops 10000000000 | bytes 16777216 | tf_op jit(solution)/shard_map/blockgrad1/pallas_call | solution.py:482
  107.3 0.2 all-to-all-done.3.back_ref
  107.6 0.0 copy-done.1
  107.6 0.0 copy-done.3
  107.6 9.7 %final.1 = (bf16[1024,1024]{1,0:T(8,128)(2,1)}, bf16[1024,1024]{1,0:T(8,128)(2,1)}, f32[8,1,128]{2,1,0:T(1,128)}) custom-call(bf16[1024,1024]{1,0:T(8,128)(2,1)} %k_ref.7, bf16[1024,1024]{1,0:T(8,128)(2,1)} %v_ref.7, f32[1024,1024]{1,0:T(8,128)} %get-tuple-element.51.c_ref, f32[8,8,128]{2,1,0:T(8,128)S(1)} %copy-done.1, ...), custom_call_target="tpu_custom_call" | custom-call | bytes 16777216 | tf_op jit(solution)/shard_map/final/pallas_call | solution.py:501
Async XLA Ops:
  7.8 21.8 %all-to-all-start = ((f32[32,40,128]{2,1,0:T(8,128)}), f32[32,40,128]{2,1,0:T(8,128)S(1)}, u32[]{:S(2)}, u32[]{:S(2)}) async-start(f32[32,40,128]{2,1,0:T(8,128)} %state.1), calls=%async_computation | async-start | bytes 1310720 | tf_op jit(solution)/shard_map/all_to_all | solution.py:432
  30.7 15.9 %all-to-all-start.1 = ((f32[32,32,128]{2,1,0:T(8,128)}), f32[32,32,128]{2,1,0:T(8,128)S(1)}, u32[]{:S(2)}, u32[]{:S(2)}) async-start(f32[32,32,128]{2,1,0:T(8,128)} %fscan.1), calls=%async_computation.1 | async-start | bytes 1048576 | tf_op jit(solution)/shard_map/all_to_all | solution.py:459
  35.5 11.1 %copy-start.2 = (f32[1024]{0:T(1024)S(1)}, f32[1024]{0:T(1024)}, u32[]{:S(2)}) copy-start(f32[1024]{0:T(1024)} %param.12) | copy-start | bytes 12292
  35.5 11.1 %copy-start.4 = (f32[1024]{0:T(1024)S(1)}, f32[1024]{0:T(1024)}, u32[]{:S(2)}) copy-start(f32[1024]{0:T(1024)} %param.13) | copy-start | bytes 12292
  46.6 6.9 %copy-start = (f32[32,32,128]{2,1,0:T(8,128)}, f32[32,32,128]{2,1,0:T(8,128)S(1)}, u32[]{:S(2)}) copy-start(f32[32,32,128]{2,1,0:T(8,128)S(1)} %all-to-all-done.1) | copy-start | bytes 1572868
  53.6 4.1 %collective-permute-start = (f32[1,16,128]{2,1,0:T(8,128)S(1)}, f32[1,16,128]{2,1,0:T(8,128)S(1)}, u32[]{:S(2)}, u32[]{:S(2)}) collective-permute-start(f32[1,16,128]{2,1,0:T(8,128)S(1)} %get-tuple-element.58.rest_0_), channel_id=1, source_target_pairs={{0,2},{1,3},{2,0},{3,1},{4,6},{5,7},{6,4},{7,5},{8,10},{9,11},{10,... | collective-permute-start | bytes 24584 | tf_op jit(solution)/shard_map/ppermute | solution.py:469
  56.4 2.8 %collective-permute-start.1 = (f32[1,16,128]{2,1,0:T(8,128)S(1)}, f32[1,16,128]{2,1,0:T(8,128)S(1)}, u32[]{:S(2)}, u32[]{:S(2)}) collective-permute-start(f32[1,16,128]{2,1,0:T(8,128)S(1)} %get-tuple-element.58.rest_0_), channel_id=1, source_target_pairs={{0,1},{1,0},{2,3},{3,2},{4,5},{5,4},{6,7},{7,6},{8,9},{9,8},{10,11... | collective-permute-start | bytes 24584 | tf_op jit(solution)/shard_map/ppermute | solution.py:469
  56.7 3.7 %collective-permute-start.2 = (f32[1,16,128]{2,1,0:T(8,128)S(1)}, f32[1,16,128]{2,1,0:T(8,128)S(1)}, u32[]{:S(2)}, u32[]{:S(2)}) collective-permute-start(f32[1,16,128]{2,1,0:T(8,128)S(1)} %get-tuple-element.58.rest_0_), channel_id=1, source_target_pairs={{0,3},{1,2},{2,1},{3,0},{4,7},{5,6},{6,5},{7,4},{8,11},{9,10},{10,... | collective-permute-start | bytes 24584 | tf_op jit(solution)/shard_map/ppermute | solution.py:469
  65.9 20.9 %all-to-all-start.2 = ((f32[32,40,128]{2,1,0:T(8,128)}), f32[32,40,128]{2,1,0:T(8,128)S(1)}, u32[]{:S(2)}, u32[]{:S(2)}) async-start(f32[32,40,128]{2,1,0:T(8,128)} %get-tuple-element.68), calls=%async_computation.2 | async-start | bytes 1310720 | tf_op jit(solution)/shard_map/all_to_all | solution.py:478
  88.0 19.6 %all-to-all-start.3 = ((f32[32,40,128]{2,1,0:T(8,128)}), f32[32,40,128]{2,1,0:T(8,128)S(1)}, u32[]{:S(2)}, u32[]{:S(2)}) async-start(f32[32,40,128]{2,1,0:T(8,128)} %bscan.1), calls=%async_computation.3 | async-start | bytes 1310720 | tf_op jit(solution)/shard_map/all_to_all | solution.py:500
  95.4 12.2 %copy-start.1 = (f32[8,8,128]{2,1,0:T(8,128)S(1)}, f32[8,8,128]{2,1,0:T(8,128)}, u32[]{:S(2)}) copy-start(f32[8,8,128]{2,1,0:T(8,128)} %get-tuple-element.52.mid_ref) | copy-start | bytes 98308
  95.4 12.2 %copy-start.3 = (f32[1024]{0:T(1024)S(1)}, f32[1024]{0:T(1024)}, u32[]{:S(2)}) copy-start(f32[1024]{0:T(1024)} %param.12) | copy-start | bytes 12292

commit v3 on v2

--- a/solution.py
+++ b/solution.py
@@ -467,7 +467,7 @@
     )(*hbm(qd, local, out_grad), state_in, rate, gain)
     all_sums = [sums] + [
         lax.ppermute(sums, "head", [(i, i ^ step) for i in range(head_count)])
-        for step in (2, 1, 3)
+        for step in (1, 3, 2)
     ]
     back_pay, factor, core = call(
         functools.partial(grad_kernel, blocks), "grad",

time: 118 us -> 118 us (level)
  transfers between devices with their start and end apart: 7 -> 7, of which waited for: 6 -> 5; matrix products, arithmetic and copies ran while one was open for 0% -> 0% of each run, Pallas kernels for 38% -> 38%
where the time goes in v3:
time: 118 us; the launch traced here: 117 us
  Pallas kernels  75.9 us (64%)
  starting transfers between devices  33.1 us (28%)
  waiting for transfers between devices  7.66 us (6%)
    pallas_call x2, Pallas kernels, on_device(): call(functools.partial(block_grad_kernel, blocks, len(made)), f'blockgrad...  25.1 us
    pallas_call x2, Pallas kernels, on_device(): call(functools.partial(local_kernel, blocks, len(made)), f'local{part}',...  19.2 us
    pallas_call x1, Pallas kernels, on_device(): call(functools.partial(final_kernel, blocks), 'final', [wide, wide, wide,...  9.65 us
    all_to_all x1, starting transfers between devices, on_device(): got = lax.all_to_all(pay, around, 0, 0)  9.6 us
    all_to_all x1, starting transfers between devices, on_device(): back_got = lax.all_to_all(back_pay, around, 0, 0)  7.62 us
    all_to_all x1, starting transfers between devices, on_device(): back_in = lax.all_to_all(back_prefixes, around, 0, 0)  7.37 us
    pallas_call x1, Pallas kernels, on_device(): call(functools.partial(state_kernel, blocks), 'state', [wide, wide, wide,...  7.16 us
    pallas_call x1, Pallas kernels, on_device(): call(functools.partial(core_kernel, blocks, turns), 'core', [pair, wide,...  6.93 us
  transfers between devices with their start and end apart: 7, of which 5 were waited for; matrix products, arithmetic and copies ran while one was open for 0% of the time, Pallas kernels for 38%

profile of v3, /device:TPU:1, one launch (start us, length us, event | category | flops | bytes accessed | tf_op | source)
XLA Modules:
  0.0 117.5 jit_solution(2699607578579738998)
XLA Ops:
  0.6 7.2 %state.1 = f32[32,40,128]{2,1,0:T(8,128)} custom-call(bf16[1024,1024]{1,0:T(8,128)(2,1)} %k_ref.7, bf16[1024,1024]{1,0:T(8,128)(2,1)} %v_ref.7, f32[1024,1024]{1,0:T(8,128)} %ld_ref.5, f32[8,1,128]{2,1,0:T(1,128)} %bitcast.7), custom_call_target="tpu_custom_call" | custom-call | bytes 16777216 | tf_op jit(solution)/shard_map/state/pallas_call | solution.py:427
  7.8 9.6 %all-to-all-start = ((f32[32,40,128]{2,1,0:T(8,128)}), f32[32,40,128]{2,1,0:T(8,128)S(1)}, u32[]{:S(2)}, u32[]{:S(2)}) async-start(f32[32,40,128]{2,1,0:T(8,128)} %state.1), calls=%async_computation | async-start | bytes 1310720 | tf_op jit(solution)/shard_map/all_to_all | solution.py:432
  17.4 9.6 %local0.1 = (f32[1024,1024]{1,0:T(8,128)}, bf16[1024,2048]{1,0:T(8,128)(2,1)}, f32[8,8,128,128]{3,2,1,0:T(8,128)}, f32[1024,1024]{1,0:T(8,128)}, f32[8,8,128]{2,...) custom-call(bf16[1024,1024]{1,0:T(8,128)(2,1)} %q_ref.3, ...), custom_call_target="tpu_custom_call" | custom-call | flops 10000000000 | bytes 16777216 | tf_op jit(solution)/shard_map/local0/pallas_call | solution.py:437
  27.0 2.6 %all-to-all-done.pay_ref.extra_ref = f32[32,40,128]{2,1,0:T(8,128)S(1)} async-done(((f32[32,40,128]{2,1,0:T(8,128)}), f32[32,40,128]{2,1,0:T(8,128)S(1)}, u32[]{:S(2)}, u32[]{:S(2)}) %all-to-all-start) | async-done | bytes 655392 | tf_op jit(solution)/shard_map/all_to_all | solution.py:432
  29.6 1.2 fscan.1
  30.7 4.8 %all-to-all-start.1 = ((f32[32,32,128]{2,1,0:T(8,128)}), f32[32,32,128]{2,1,0:T(8,128)S(1)}, u32[]{:S(2)}, u32[]{:S(2)}) async-start(f32[32,32,128]{2,1,0:T(8,128)} %fscan.1), calls=%async_computation.1 | async-start | bytes 1048576 | tf_op jit(solution)/shard_map/all_to_all | solution.py:459
  35.5 0.0 copy-start.2
  35.5 0.0 copy-start.4
  35.6 9.6 %local1.1 = (f32[1024,1024]{1,0:T(8,128)}, bf16[1024,2048]{1,0:T(8,128)(2,1)}, f32[8,8,128,128]{3,2,1,0:T(8,128)}, f32[1024,1024]{1,0:T(8,128)}, f32[8,8,128]{2,...) custom-call(bf16[1024,1024]{1,0:T(8,128)(2,1)} %q_ref.3, ...), custom_call_target="tpu_custom_call", output_to_operand_aliasing={{0}: (5, {}), {1}: (6, {}), {2}: (7, {}), {3}: (8, {}), {4}... | custom-call | flops 10000000000 | bytes 16777216 | tf_op jit(solution)/shard_map/local1/pallas_call | solution.py:437
  45.2 1.5 %all-to-all-done.1 = f32[32,32,128]{2,1,0:T(8,128)S(1)} async-done(((f32[32,32,128]{2,1,0:T(8,128)}), f32[32,32,128]{2,1,0:T(8,128)S(1)}, u32[]{:S(2)}, u32[]{:S(2)}) %all-to-all-start.1) | async-done | bytes 524320 | tf_op jit(solution)/shard_map/all_to_all | solution.py:459
  46.6 0.0 copy-start
  46.6 0.0 copy-done.2
  46.6 0.0 copy-done.4
  46.6 6.9 %core.1 = (f32[1024,1024]{1,0:T(8,128)S(1)}, bf16[1024,2048]{1,0:T(8,128)(2,1)S(1)}, bf16[1024,1024]{1,0:T(8,128)(2,1)S(1)}, f32[1,16,128]{2,1,0:T(8,128)S(1)}) custom-call(bf16[1024,2048]{1,0:T(8,128)(2,1)} %get-tuple-element.53.qd_ref, f32[1024,1024]{1,0:T(8,128)} %get-tuple-element.54.local_ref, bf16[1024,1024]{1,0:T(8,128)(2,1)} %grad_ref.5, ...), custom_call_target="tpu_custom_call" | custom-call | bytes 16777216 | tf_op jit(solution)/shard_map/core/pallas_call | solution.py:460
  53.6 0.0 copy-done
  53.6 1.3 %collective-permute-start = (f32[1,16,128]{2,1,0:T(8,128)S(1)}, f32[1,16,128]{2,1,0:T(8,128)S(1)}, u32[]{:S(2)}, u32[]{:S(2)}) collective-permute-start(f32[1,16,128]{2,1,0:T(8,128)S(1)} %get-tuple-element.58.rest_0_), channel_id=1, source_target_pairs={{0,1},{1,0},{2,3},{3,2},{4,5},{5,4},{6,7},{7,6},{8,9},{9,8},{10,11... | collective-permute-start | bytes 24584 | tf_op jit(solution)/shard_map/ppermute | solution.py:469
  54.9 1.8 %collective-permute-start.1 = (f32[1,16,128]{2,1,0:T(8,128)S(1)}, f32[1,16,128]{2,1,0:T(8,128)S(1)}, u32[]{:S(2)}, u32[]{:S(2)}) collective-permute-start(f32[1,16,128]{2,1,0:T(8,128)S(1)} %get-tuple-element.58.rest_0_), channel_id=1, source_target_pairs={{0,3},{1,2},{2,1},{3,0},{4,7},{5,6},{6,5},{7,4},{8,11},{9,10},{10,... | collective-permute-start | bytes 24584 | tf_op jit(solution)/shard_map/ppermute | solution.py:469
  56.7 0.6 collective-permute-start.2
  57.3 0.0 collective-permute-done.rest_1_
  57.3 1.3 %collective-permute-done.1.rest_2_ = f32[1,16,128]{2,1,0:T(8,128)S(1)} collective-permute-done((f32[1,16,128]{2,1,0:T(8,128)S(1)}, f32[1,16,128]{2,1,0:T(8,128)S(1)}, u32[]{:S(2)}, u32[]{:S(2)}) %collective-permute-start.1) | collective-permute-done | bytes 8224 | tf_op jit(solution)/shard_map/ppermute | solution.py:469
  58.6 2.1 %collective-permute-done.2.rest_3_ = f32[1,16,128]{2,1,0:T(8,128)S(1)} collective-permute-done((f32[1,16,128]{2,1,0:T(8,128)S(1)}, f32[1,16,128]{2,1,0:T(8,128)S(1)}, u32[]{:S(2)}, u32[]{:S(2)}) %collective-permute-start.2) | collective-permute-done | bytes 8224 | tf_op jit(solution)/shard_map/ppermute | solution.py:469
  60.7 5.5 %grad.1 = (f32[32,40,128]{2,1,0:T(8,128)}, f32[1024,256]{1,0:T(8,128)}, f32[1024,1024]{1,0:T(8,128)}) custom-call(bf16[1024,2048]{1,0:T(8,128)(2,1)S(1)} %get-tuple-element.55.qd_ref, f32[1024,1024]{1,0:T(8,128)S(1)} %get-tuple-element.56.core_ref, bf16[1024,1024]{1,0:T(8,128)(2,1)S(1)} %get-tuple-element.57.grad_ref, f32[8,1,128]{2,1,0:T(1,128)S(1)} %bitcast.13, ...), custom_call_target="tpu_custom_call" | custom-call | bytes 16777216 | tf_op jit(solution)/shard_map/grad/pallas_call | solution.py:472
  66.2 7.6 %all-to-all-start.2 = ((f32[32,40,128]{2,1,0:T(8,128)}), f32[32,40,128]{2,1,0:T(8,128)S(1)}, u32[]{:S(2)}, u32[]{:S(2)}) async-start(f32[32,40,128]{2,1,0:T(8,128)} %get-tuple-element.68), calls=%async_computation.2 | async-start | bytes 1310720 | tf_op jit(solution)/shard_map/all_to_all | solution.py:478
  73.8 13.2 %blockgrad0.1 = (bf16[1024,1024]{1,0:T(8,128)(2,1)}, f32[1024,1024]{1,0:T(8,128)}, f32[1024,1024]{1,0:T(8,128)}) custom-call(bf16[1024,2048]{1,0:T(8,128)(2,1)} %get-tuple-element.47.qs, bf16[1024,2048]{1,0:T(8,128)(2,1)} %get-tuple-element.48.ks, bf16[1024,2048]{1,0:T(8,128)(2,1)} %get-tuple-element.49.vs, bf16[1024,2048]{1,0:T(8,128)(2,1)} %get-tuple-element.50.scores, ...), custom_call_target="tpu_custom_call" | custom-call | flops 10000000000 | bytes 16777216 | tf_op jit(solution)/shard_map/blockgrad0/pallas_call | solution.py:482
  87.1 0.0 all-to-all-done.2.pay_ref.gain_ref
  87.1 1.2 %bscan.1 = f32[32,40,128]{2,1,0:T(8,128)} custom-call(f32[32,40,128]{2,1,0:T(8,128)S(1)} %all-to-all-done.2.pay_ref.gain_ref, f32[32,40,128]{2,1,0:T(8,128)S(1)} %all-to-all-done.2.pay_ref.gain_ref, f32[32,40,128]{2,1,0:T(8,128)S(1)} %all-to-all-done.pay_ref.extra_ref), custom_call_target="tpu_custom_call" | custom-call | tf_op jit(solution)/shard_map/bscan/pallas_call | solution.py:495
  88.3 7.4 %all-to-all-start.3 = ((f32[32,40,128]{2,1,0:T(8,128)}), f32[32,40,128]{2,1,0:T(8,128)S(1)}, u32[]{:S(2)}, u32[]{:S(2)}) async-start(f32[32,40,128]{2,1,0:T(8,128)} %bscan.1), calls=%async_computation.3 | async-start | bytes 1310720 | tf_op jit(solution)/shard_map/all_to_all | solution.py:500
  95.7 0.0 copy-start.1
  95.7 0.0 copy-start.3
  95.7 11.9 %blockgrad1.1 = (bf16[1024,1024]{1,0:T(8,128)(2,1)}, f32[1024,1024]{1,0:T(8,128)}, f32[1024,1024]{1,0:T(8,128)}) custom-call(bf16[1024,2048]{1,0:T(8,128)(2,1)} %get-tuple-element.47.qs, bf16[1024,2048]{1,0:T(8,128)(2,1)} %get-tuple-element.48.ks, ...), custom_call_target="tpu_custom_call", output_to_operand_aliasing={{0}: (13, {}), {1}: (14, {}), {2}: (15, {})} | custom-call | flops 10000000000 | bytes 16777216 | tf_op jit(solution)/shard_map/blockgrad1/pallas_call | solution.py:482
  107.6 0.2 all-to-all-done.3.back_ref
  107.8 0.0 copy-done.1
  107.8 0.0 copy-done.3
  107.8 9.7 %final.1 = (bf16[1024,1024]{1,0:T(8,128)(2,1)}, bf16[1024,1024]{1,0:T(8,128)(2,1)}, f32[8,1,128]{2,1,0:T(1,128)}) custom-call(bf16[1024,1024]{1,0:T(8,128)(2,1)} %k_ref.7, bf16[1024,1024]{1,0:T(8,128)(2,1)} %v_ref.7, f32[1024,1024]{1,0:T(8,128)} %get-tuple-element.51.c_ref, f32[8,8,128]{2,1,0:T(8,128)S(1)} %copy-done.1, ...), custom_call_target="tpu_custom_call" | custom-call | bytes 16777216 | tf_op jit(solution)/shard_map/final/pallas_call | solution.py:501
Async XLA Ops:
  7.8 21.8 %all-to-all-start = ((f32[32,40,128]{2,1,0:T(8,128)}), f32[32,40,128]{2,1,0:T(8,128)S(1)}, u32[]{:S(2)}, u32[]{:S(2)}) async-start(f32[32,40,128]{2,1,0:T(8,128)} %state.1), calls=%async_computation | async-start | bytes 1310720 | tf_op jit(solution)/shard_map/all_to_all | solution.py:432
  30.7 15.9 %all-to-all-start.1 = ((f32[32,32,128]{2,1,0:T(8,128)}), f32[32,32,128]{2,1,0:T(8,128)S(1)}, u32[]{:S(2)}, u32[]{:S(2)}) async-start(f32[32,32,128]{2,1,0:T(8,128)} %fscan.1), calls=%async_computation.1 | async-start | bytes 1048576 | tf_op jit(solution)/shard_map/all_to_all | solution.py:459
  35.5 11.1 %copy-start.2 = (f32[1024]{0:T(1024)S(1)}, f32[1024]{0:T(1024)}, u32[]{:S(2)}) copy-start(f32[1024]{0:T(1024)} %param.12) | copy-start | bytes 12292
  35.5 11.1 %copy-start.4 = (f32[1024]{0:T(1024)S(1)}, f32[1024]{0:T(1024)}, u32[]{:S(2)}) copy-start(f32[1024]{0:T(1024)} %param.13) | copy-start | bytes 12292
  46.6 6.9 %copy-start = (f32[32,32,128]{2,1,0:T(8,128)}, f32[32,32,128]{2,1,0:T(8,128)S(1)}, u32[]{:S(2)}) copy-start(f32[32,32,128]{2,1,0:T(8,128)S(1)} %all-to-all-done.1) | copy-start | bytes 1572868
  53.6 3.7 %collective-permute-start = (f32[1,16,128]{2,1,0:T(8,128)S(1)}, f32[1,16,128]{2,1,0:T(8,128)S(1)}, u32[]{:S(2)}, u32[]{:S(2)}) collective-permute-start(f32[1,16,128]{2,1,0:T(8,128)S(1)} %get-tuple-element.58.rest_0_), channel_id=1, source_target_pairs={{0,1},{1,0},{2,3},{3,2},{4,5},{5,4},{6,7},{7,6},{8,9},{9,8},{10,11... | collective-permute-start | bytes 24584 | tf_op jit(solution)/shard_map/ppermute | solution.py:469
  54.9 3.7 %collective-permute-start.1 = (f32[1,16,128]{2,1,0:T(8,128)S(1)}, f32[1,16,128]{2,1,0:T(8,128)S(1)}, u32[]{:S(2)}, u32[]{:S(2)}) collective-permute-start(f32[1,16,128]{2,1,0:T(8,128)S(1)} %get-tuple-element.58.rest_0_), channel_id=1, source_target_pairs={{0,3},{1,2},{2,1},{3,0},{4,7},{5,6},{6,5},{7,4},{8,11},{9,10},{10,... | collective-permute-start | bytes 24584 | tf_op jit(solution)/shard_map/ppermute | solution.py:469
  56.7 4.0 %collective-permute-start.2 = (f32[1,16,128]{2,1,0:T(8,128)S(1)}, f32[1,16,128]{2,1,0:T(8,128)S(1)}, u32[]{:S(2)}, u32[]{:S(2)}) collective-permute-start(f32[1,16,128]{2,1,0:T(8,128)S(1)} %get-tuple-element.58.rest_0_), channel_id=1, source_target_pairs={{0,2},{1,3},{2,0},{3,1},{4,6},{5,7},{6,4},{7,5},{8,10},{9,11},{10,... | collective-permute-start | bytes 24584 | tf_op jit(solution)/shard_map/ppermute | solution.py:469
  66.2 20.9 %all-to-all-start.2 = ((f32[32,40,128]{2,1,0:T(8,128)}), f32[32,40,128]{2,1,0:T(8,128)S(1)}, u32[]{:S(2)}, u32[]{:S(2)}) async-start(f32[32,40,128]{2,1,0:T(8,128)} %get-tuple-element.68), calls=%async_computation.2 | async-start | bytes 1310720 | tf_op jit(solution)/shard_map/all_to_all | solution.py:478
  88.3 19.6 %all-to-all-start.3 = ((f32[32,40,128]{2,1,0:T(8,128)}), f32[32,40,128]{2,1,0:T(8,128)S(1)}, u32[]{:S(2)}, u32[]{:S(2)}) async-start(f32[32,40,128]{2,1,0:T(8,128)} %bscan.1), calls=%async_computation.3 | async-start | bytes 1310720 | tf_op jit(solution)/shard_map/all_to_all | solution.py:500
  95.7 12.2 %copy-start.1 = (f32[8,8,128]{2,1,0:T(8,128)S(1)}, f32[8,8,128]{2,1,0:T(8,128)}, u32[]{:S(2)}) copy-start(f32[8,8,128]{2,1,0:T(8,128)} %get-tuple-element.52.mid_ref) | copy-start | bytes 98308
  95.7 12.2 %copy-start.3 = (f32[1024]{0:T(1024)S(1)}, f32[1024]{0:T(1024)}, u32[]{:S(2)}) copy-start(f32[1024]{0:T(1024)} %param.12) | copy-start | bytes 12292
